TPU v7x, 32 devices: a whole 2x2x4 slice. The times are simulated.
32 devices in a mesh: sec: 2 (over x), ep: 4 (over z), tp: 4 (over y, core).
Axes of the slice: x: 2, y: 2, z: 4, core: 2. Of those that a mesh axis runs over, the one named last changes fastest.
Arguments:
- queries: bfloat16 [32, 64, 576], P(('sec', 'ep'), 'tp')
- cache: bfloat16 [32, 32, 576], P(('sec', 'ep'))
- lengths: int32 [32], P(('sec', 'ep')), may hold values from 2 to 32, as said below
- w_uv: bfloat16 [64, 512, 128], P('tp'), may hold values from -0.25 to 0.25
- w_out: bfloat16 [8192, 7168], P('tp', 'ep'), may hold values from -0.0625 to 0.0625
- residual: bfloat16 [32, 7168], P(('sec', 'ep'), 'tp')
- gain: float32 [7168], P('tp'), may hold values from 0.5 to 1.5
- expert_ids: int32 [32, 4], P(('sec', 'ep')), may hold values from 0 to 15, all different within a row; in each aligned block of 4 rows (0 to 3, 4 to 7, ...) at most 2 rows name the same one
- expert_weights: float32 [32, 4], P(('sec', 'ep')), may hold values from 0.2 to 1
- w_gate: bfloat16 [128, 7168, 256], P(('sec', 'ep'), 'tp'), may hold values from -0.0625 to 0.0625
- w_up: bfloat16 [128, 7168, 256], P(('sec', 'ep'), 'tp'), may hold values from -0.0625 to 0.0625
- w_down: bfloat16 [128, 256, 7168], P(('sec', 'ep'), None, 'tp'), may hold values from -0.125 to 0.125
Outputs:
- next_state: bfloat16 [32, 7168], P(('sec', 'ep'), 'tp')
Inputs may be any that keep to these rules, and one draw needn't show every extreme that they name: `expert_ids`: within each device's rows (aligned blocks of 4 requests) no expert is named by more than 2 routes, a bound that some block reaches. `lengths`: the first request of each aligned block of 4 requests has all 32 positions live.
All inputs are finite; a program needn't handle non-finite values.
Results may differ from a plain program's by a relative error of at most 0.0058.
Values may be sent and summed in bfloat16 or wider, within the bound.
No kernel may reach another device: no remote copies, remote signals or barrier semaphores. Data moves between devices by JAX's collectives and lax.ppermute only.
A program may use at most 128 MiB of HBM per device.

v0:
```python
import jax
import jax.numpy as jnp
from jax import lax
from jax.sharding import PartitionSpec as P

D = 7168
HSPLIT = 8
EXPERTS = 16
CAP = 2


score_scale = 0.07216878364870322
norm_eps = 1e-06


def local(
    queries,
    cache,
    lengths,
    w_uv,
    w_out,
    residual,
    gain,
    expert_ids,
    expert_weights,
    w_gate,
    w_up,
    w_down,
):
    req_rows = queries.shape[0]
    latent_width = w_uv.shape[1]
    scores = (
        jnp.einsum("rhc,rlc->rhl", queries, cache, preferred_element_type=jnp.float32) * score_scale
    )
    positions = lax.broadcasted_iota(jnp.int32, scores.shape, 2)
    live_mask = positions < lengths[:, None, None]
    scores = jnp.where(live_mask, scores, -1e30)
    row_top = jnp.max(scores, axis=-1, keepdims=True)
    raw_weights = jnp.where(live_mask, jnp.exp(scores - row_top), 0.0)
    probs = (raw_weights / jnp.sum(raw_weights, axis=-1, keepdims=True)).astype(jnp.bfloat16)
    latent = jnp.einsum(
        "rhl,rlc->rhc", probs, cache[:, :, :latent_width], preferred_element_type=jnp.float32
    ).astype(jnp.bfloat16)
    values = jnp.einsum("rhc,hcv->rhv", latent, w_uv, preferred_element_type=jnp.float32).astype(
        jnp.bfloat16
    )
    values = values.reshape(req_rows, -1)
    projected = jnp.dot(
        lax.all_gather(values, "ep", axis=0, tiled=True), w_out, preferred_element_type=jnp.float32
    )
    full_rows = lax.all_to_all(projected, "ep", split_axis=0, concat_axis=1, tiled=True)
    attention = lax.psum_scatter(full_rows, "tp", scatter_dimension=1, tiled=True)
    hidden_state = (residual.astype(jnp.float32) + attention).astype(jnp.bfloat16)
    column_count = hidden_state.shape[1]
    topk_count = expert_ids.shape[1]
    flat_ids = expert_ids.reshape(-1)
    onehot = (flat_ids[:, None] == jnp.arange(EXPERTS, dtype=jnp.int32)[None, :]).astype(jnp.int32)
    rank = jnp.sum((jnp.cumsum(onehot, axis=0) - onehot) * onehot, axis=1)
    slot_index = flat_ids * CAP + rank
    route_rows = jnp.repeat(hidden_state, topk_count, axis=0)
    slot_table = (
        jnp.zeros((EXPERTS * CAP, column_count), jnp.bfloat16).at[slot_index].set(route_rows)
    )
    sending = jnp.repeat(slot_table.reshape(EXPERTS, CAP, column_count), HSPLIT, axis=0)
    sec_count = lax.axis_size("sec")
    ep_count = lax.axis_size("ep")
    groups = sec_count * ep_count
    local_pieces = w_gate.shape[0]
    sending = sending.reshape(groups, local_pieces * CAP, column_count)
    received = lax.all_to_all(sending, ("sec", "ep"), split_axis=0, concat_axis=0, tiled=True)
    arrived = received.reshape(groups, local_pieces, CAP, column_count)
    arrived_wide = arrived.astype(jnp.float32)
    squares = jnp.sum(arrived_wide * arrived_wide, axis=-1)
    scaled = (arrived_wide * gain[None, None, None, :]).astype(jnp.bfloat16)
    gate_part = jnp.einsum("gpcd,pdh->gpch", scaled, w_gate, preferred_element_type=jnp.float32)
    up_part = jnp.einsum("gpcd,pdh->gpch", scaled, w_up, preferred_element_type=jnp.float32)
    gate_part, up_part, squares = lax.psum((gate_part, up_part, squares), "tp")
    inv_rms = lax.rsqrt(squares / D + norm_eps)[..., None]
    activated = (jax.nn.silu(gate_part * inv_rms) * (up_part * inv_rms)).astype(jnp.bfloat16)
    piece_out = jnp.einsum(
        "gpch,phd->gpcd", activated, w_down, preferred_element_type=jnp.float32
    ).astype(jnp.bfloat16)
    returned = lax.all_to_all(
        piece_out.reshape(groups, local_pieces * CAP, column_count),
        ("sec", "ep"),
        split_axis=0,
        concat_axis=0,
        tiled=True,
    )
    per_expert = jnp.sum(
        returned.reshape(EXPERTS, HSPLIT, CAP, column_count).astype(jnp.float32), axis=1
    )
    route_out = per_expert.reshape(EXPERTS * CAP, column_count)[slot_index]
    mixture = jnp.sum(
        route_out.reshape(req_rows, topk_count, column_count) * expert_weights[:, :, None], axis=1
    )
    return (hidden_state.astype(jnp.float32) + mixture).astype(jnp.bfloat16)


def solution(mesh):
    in_specs = (
        P(("sec", "ep"), "tp", None),
        P(("sec", "ep"), None, None),
        P(("sec", "ep")),
        P("tp", None, None),
        P("tp", "ep"),
        P(("sec", "ep"), "tp"),
        P("tp"),
        P(("sec", "ep"), None),
        P(("sec", "ep"), None),
        P(("sec", "ep"), "tp", None),
        P(("sec", "ep"), "tp", None),
        P(("sec", "ep"), None, "tp"),
    )
    out_specs = P(("sec", "ep"), "tp")
    return jax.shard_map(local, mesh=mesh, in_specs=in_specs, out_specs=out_specs, check_vma=False)
```

profile of v0, /device:TPU:0, one launch (start us, length us, event | category | flops | bytes accessed | tf_op | source)
XLA Modules:
  0.0 211.9 jit_solution(13415633587053292233)
XLA Ops:
  6.5 1.3 fusion.19
  7.8 0.8 fusion.33
  8.7 1.2 convolution_convert_fusion
  9.9 0.0 copy-done
  9.9 0.4 fusion.20
  10.2 14.9 %all-gather = bf16[4,4,2048]{2,1,0:T(4,128)(2,1)S(1)} all-gather(bf16[1,4,2048]{2,1,0:T(4,128)(2,1)S(1)} %fusion.20), channel_id=1, replica_groups=mesh['sec'=2,'ep'=4,'tp'=4] {'ep'}, dimensions={0}, use_global_device_ids=true | all-gather | bytes 81920 | tf_op jit(solution)/shard_map/all_gather | solution.py:49
  25.2 0.0 copy-start.4
  25.2 4.1 %fusion.34 = f32[16,1792]{1,0:T(8,128)S(1)} fusion(bf16[16,2048]{1,0:T(8,128)(2,1)S(1)} %reshape.89, bf16[2048,1792]{1,0:T(8,128)(2,1)} %param.16), kind=kOutput, calls=%fused_computation.48 | convolution fusion | flops 117440512 | bytes 7520256 | tf_op jit(solution)/shard_map/dot_general | solution.py:48
  29.3 0.7 all_to_all.20
  30.0 4.7 %all-to-all-start = ((f32[4,4,1792]{2,1,0:T(4,128)}), f32[4,4,1792]{2,1,0:T(4,128)S(1)}, u32[]{:S(2)}, u32[]{:S(2)}) async-start(f32[4,4,1792]{2,1,0:T(4,128)} %all_to_all.20), calls=%async_computation | async-start | bytes 229376 | tf_op jit(solution)/shard_map/all_to_all | solution.py:51
  34.7 0.0 reduce-scatter.4.cloned.1.call-start
  34.7 0.1 eq.15
  34.8 0.1 fusion.28
  34.9 5.7 %all-to-all-done = f32[4,4,1792]{2,1,0:T(4,128)S(1)} async-done(((f32[4,4,1792]{2,1,0:T(4,128)}), f32[4,4,1792]{2,1,0:T(4,128)S(1)}, u32[]{:S(2)}, u32[]{:S(2)}) %all-to-all-start) | async-done | bytes 114720 | tf_op jit(solution)/shard_map/all_to_all | solution.py:51
  40.6 2.4 %copy.38 = f32[4,7168]{0,1:T(8,128)} copy(f32[4,7168]{1,0:T(4,128)S(1)} %bitcast.57) | data formatting | bytes 229376
  43.0 0.0 reduce-scatter.4.cloned.1.call-update
  43.0 0.0 all-reduce.3.cloned.1.call-start
  43.1 0.2 select_reduce_fusion
  43.3 0.1 mul.66
  43.4 40.0 %reduce-scatter.4.cloned.1.call-done = f32[1792,4]{1,0:T(8,128)} async-done(((f32[7168,4]{1,0:T(8,128)}), f32[1792,4]{1,0:T(8,128)}) %reduce-scatter.4.cloned.1.call-update) | async-done | bytes 28688
  83.4 1.5 copy.39
  84.9 0.0 copy-done.3
  84.9 0.7 scatter_custom_fusion
  85.7 0.0 copy-start.2
  85.7 0.5 broadcast_in_dim.29
  86.2 0.3 reshape_reshape.3
  86.6 29.1 %all_to_all.29 = bf16[8,32,1792]{2,1,0:T(8,128)(2,1)S(1)} all-to-all(bf16[8,32,1792]{2,1,0:T(8,128)(2,1)S(1)} %reshape_reshape.3), channel_id=1, replica_groups=mesh['sec'=2,'ep'=4,'tp'=4] {'sec','ep'}, dimensions={0} | all-to-all | bytes 1835008 | tf_op jit(solution)/shard_map/all_to_all | solution.py:70
  115.7 0.5 copy.37
  116.2 8.0 %fusion.10 = f32[8,16,2,256]{3,0,2,1:T(8,128)} fusion(bf16[16,1792,256]{2,1,0:T(8,128)(2,1)} %param.21, f32[8,16,2,1792]{3,0,2,1:T(8,128)S(1)} %bitcast.52, f32[1792]{0:T(1024)S(1)} %copy-done.2), kind=kOutput, calls=%fused_computation.12 | convolution fusion | flops 235798528 | bytes 16784384 | tf_op jit(solution)/shard_map/gpcd,pdh->gpch/dot_general | solution.py:75
  124.2 7.9 %fusion.13 = f32[8,16,2,256]{3,0,2,1:T(8,128)} fusion(bf16[16,1792,256]{2,1,0:T(8,128)(2,1)} %param.22, f32[8,16,2,1792]{3,0,2,1:T(8,128)S(1)} %bitcast.53, f32[1792]{0:T(1024)S(1)} %copy-done.2), kind=kOutput, calls=%fused_computation.13 | convolution fusion | flops 235798528 | bytes 16784384 | tf_op jit(solution)/shard_map/gpcd,pdh->gpch/dot_general | solution.py:76
  132.1 0.0 all-reduce.3.cloned.1.call-update
  132.1 0.3 multiply_reduce_fusion
  132.4 0.1 copy.30
  132.5 0.1 copy.31
  132.5 6.2 %psum.22 = f32[8,16,2]{1,0,2:T(8,128)S(1)} all-reduce(f32[8,16,2]{1,0,2:T(8,128)S(1)} %copy.31), channel_id=1, replica_groups=mesh['sec'=2,'ep'=4,'tp'=4] {'tp'}, use_global_device_ids=true, to_apply=%region_8.9 | all-reduce | flops 256 | bytes 2048 | tf_op jit(solution)/shard_map/psum | solution.py:77
  138.8 0.1 copy.32
  138.9 23.3 %all-reduce.3.cloned.1.call-done = (f32[8,16,2,256]{3,0,2,1:T(8,128)}, f32[8,16,2,256]{3,0,2,1:T(8,128)}) async-done(((f32[8,16,2,256]{3,0,2,1:T(8,128)}, f32[8,16,2,256]{3,0,2,1:T(8,128)}), (f32[8,16,2,256]{3,0,2,1:T(8,128)}, f32[8,16,2,256]{3,0,2,1:T(8,128)})) %all-reduce.3.cloned.1.call-update) | async-done | bytes 524304 | tf_op jit(solution)/shard_map/psum | solution.py:77
  162.2 7.4 %fusion.7 = bf16[16,8,2,1792]{3,1,2,0:T(8,128)(2,1)S(1)} fusion(bf16[16,256,1792]{2,1,0:T(8,128)(2,1)} %param.23, f32[8,16,2,256]{3,0,2,1:T(8,128)} %get-tuple-element.5, f32[8,16,2,256]{3,0,2,1:T(8,128)} %get-tuple-element.6, f32[8,16,2]{0,2,1:T(2,128)S(1)} %copy.32), kind=kOutput, calls=%fused_computation.9 | convolution fusion | flops 235864064 | bytes 16122880 | tf_op jit(solution)/shard_map/gpch,phd->gpcd/dot_general | solution.py:80
  169.6 1.1 copy.33
  170.7 5.5 %all-to-all-start.2 = ((bf16[8,32,1792]{2,1,0:T(8,128)(2,1)}), bf16[8,32,1792]{2,1,0:T(8,128)(2,1)S(1)}, u32[]{:S(2)}, u32[]{:S(2)}) async-start(bf16[8,32,1792]{2,1,0:T(8,128)(2,1)} %copy.33), calls=%async_computation.2 | async-start | bytes 1835008 | tf_op jit(solution)/shard_map/all_to_all | solution.py:83
  176.2 0.0 copy-start.1
  176.3 22.9 %all-to-all-done.2 = bf16[8,32,1792]{2,1,0:T(8,128)(2,1)S(1)} async-done(((bf16[8,32,1792]{2,1,0:T(8,128)(2,1)}), bf16[8,32,1792]{2,1,0:T(8,128)(2,1)S(1)}, u32[]{:S(2)}, u32[]{:S(2)}) %all-to-all-start.2) | async-done | bytes 917536 | tf_op jit(solution)/shard_map/all_to_all | solution.py:83
  199.1 2.1 %reshape.71 = f32[16,8,2,1792]{3,2,1,0:T(2,128)} reshape(bf16[8,32,1792]{2,1,0:T(8,128)(2,1)S(1)} %all-to-all-done.2) | data formatting | bytes 2752512 | tf_op jit(solution)/shard_map/convert_element_type | solution.py:91
  201.3 2.2 %reduce_sum.54 = f32[16,2,1792]{2,1,0:T(2,128)S(1)} reduce(f32[16,8,2,1792]{3,2,1,0:T(2,128)} %reshape.71, f32[]{:T(128)} %constant.6.clone.1), dimensions={1}, to_apply=%region_10.11 | reduce | flops 401408 | bytes 2064388 | tf_op jit(solution)/shard_map/reduce_sum | solution.py:90
  203.5 0.2 reshape.68
  203.7 0.6 gather_fusion
  204.3 0.1 multiply_reduce_fusion.1
  204.5 0.6 add_convert_fusion
  (18 shorter events, 0.2 us)
Async XLA Ops:
  6.5 3.3 %copy-start = (bf16[16,512,128]{2,1,0:T(8,128)(2,1)S(1)}, bf16[16,512,128]{2,1,0:T(8,128)(2,1)}, u32[]{:S(2)}) copy-start(bf16[16,512,128]{2,1,0:T(8,128)(2,1)} %param.15) | copy-start | bytes 6291460
  25.2 9.6 %copy-start.4 = (s32[4,4]{1,0:T(4,128)S(1)}, s32[4,4]{1,0:T(4,128)}, u32[]{:S(2)}) copy-start(s32[4,4]{1,0:T(4,128)} %param.19) | copy-start | bytes 196
  30.0 10.6 %all-to-all-start = ((f32[4,4,1792]{2,1,0:T(4,128)}), f32[4,4,1792]{2,1,0:T(4,128)S(1)}, u32[]{:S(2)}, u32[]{:S(2)}) async-start(f32[4,4,1792]{2,1,0:T(4,128)} %all_to_all.20), calls=%async_computation | async-start | bytes 229376 | tf_op jit(solution)/shard_map/all_to_all | solution.py:51
  34.7 48.6 %reduce-scatter.4.cloned.1.call-start = ((), (), s32[]{:S(2)}) async-start(), calls=%async_computation.4 | async-start | bytes 4587520
  40.6 44.2 %copy-start.3 = (bf16[4,1792]{1,0:T(4,128)(2,1)S(1)}, bf16[4,1792]{1,0:T(4,128)(2,1)}, u32[]{:S(2)}) copy-start(bf16[4,1792]{1,0:T(4,128)(2,1)} %param.17) | copy-start | bytes 43012
  43.0 119.1 %all-reduce.3.cloned.1.call-start = ((), (), s32[]{:S(2)}) async-start(), calls=%async_computation.5 | async-start | bytes 1048576 | tf_op jit(solution)/shard_map/psum | solution.py:77
  85.7 30.5 %copy-start.2 = (f32[1792]{0:T(1024)S(1)}, f32[1792]{0:T(1024)}, u32[]{:S(2)}) copy-start(f32[1792]{0:T(1024)} %param.18) | copy-start | bytes 21508
  170.7 28.4 %all-to-all-start.2 = ((bf16[8,32,1792]{2,1,0:T(8,128)(2,1)}), bf16[8,32,1792]{2,1,0:T(8,128)(2,1)S(1)}, u32[]{:S(2)}, u32[]{:S(2)}) async-start(bf16[8,32,1792]{2,1,0:T(8,128)(2,1)} %copy.33), calls=%async_computation.2 | async-start | bytes 1835008 | tf_op jit(solution)/shard_map/all_to_all | solution.py:83
  176.2 28.1 %copy-start.5 = (f32[4,4]{1,0:T(4,128)S(1)}, f32[4,4]{1,0:T(4,128)}, u32[]{:S(2)}) copy-start(f32[4,4]{1,0:T(4,128)} %param.20) | copy-start | bytes 196
  176.2 28.9 %copy-start.1 = (bf16[16,512,128]{2,1,0:T(8,128)(2,1)S(1)}, bf16[16,512,128]{2,1,0:T(8,128)(2,1)}, u32[]{:S(2)}) copy-start(bf16[16,512,128]{2,1,0:T(8,128)(2,1)} %param.15) | copy-start | bytes 6291460
Sparse Core Ops, SparseCore 0:
  43.2 40.1 reduce-scatter.3
  132.2 29.9 all-reduce.2
where the time goes:
time: 213 us; the launch traced here: 212 us
  waiting for transfers between devices  91.9 us (43%)
  blocking collectives  50.2 us (24%)
  matrix products  30.3 us (14%)
  between operations  13.6 us (6%)
  local copies, waits for them, and re-layouts  11.2 us (5%)
  starting transfers between devices  10.3 us (5%)
  other arithmetic  4.42 us (2%)
    unnamed x3, waiting for transfers between devices  40 us
    all_to_all x1, blocking collectives, local(): lax.all_to_all(sending, ('sec', 'ep'), split_axis=0, concat_axis=0, tiled...  29.1 us
    psum x1, waiting for transfers between devices, local(): gate_part, up_part, squares = lax.psum((gate_part, up_part, squares), 'tp')  23.3 us
    all_to_all x1, waiting for transfers between devices, local(): lax.all_to_all(piece_out.reshape(groups, local_pieces * CAP, column_count...  22.9 us
    all_gather x1, blocking collectives, local(): lax.all_gather(values, 'ep', axis=0, tiled=True)  14.9 us
    dot_general x1, matrix products, local(): jnp.einsum('gpcd,pdh->gpch', scaled, w_gate, preferred_element_type=jnp.f...  7.95 us
    dot_general x1, matrix products, local(): jnp.einsum('gpcd,pdh->gpch', scaled, w_up, preferred_element_type=jnp.flo...  7.94 us
    dot_general x1, matrix products, local(): jnp.einsum('gpch,phd->gpcd', activated, w_down, preferred_element_type=jn...  7.43 us
  transfers between devices with their start and end apart: 4, of which 4 were waited for; matrix products, arithmetic and copies ran while one was open for 0% of the time, Pallas kernels for 0%

commit v1 on v0

--- a/solution.py
+++ b/solution.py
@@ -1,6 +1,8 @@
 import jax
 import jax.numpy as jnp
 from jax import lax
+from jax.experimental import pallas as pl
+from jax.experimental.pallas import tpu as pltpu
 from jax.sharding import PartitionSpec as P
 
 D = 7168
@@ -12,8 +14,387 @@
 score_scale = 0.07216878364870322
 norm_eps = 1e-06
 
+f32 = jnp.float32
+bf16 = jnp.bfloat16
+VMEM = pl.BlockSpec(memory_space=pltpu.VMEM)
+SMEM = pl.BlockSpec(memory_space=pltpu.SMEM)
+
+
+def cost(micros):
+    return pl.CostEstimate(flops=micros * 1_000_000_000, bytes_accessed=1_000_000, transcendentals=0)
+
+
+COST0, COST1, COST2 = cost(10), cost(30), cost(60)
+
+
+def call(body, outs, args, specs, scratch=(), limit=4 << 20, cost=None):
+    return pl.pallas_call(
+        body,
+        out_shape=[jax.ShapeDtypeStruct(s, d) for s, d in outs],
+        in_specs=specs,
+        out_specs=[VMEM] * len(outs),
+        scratch_shapes=list(scratch),
+        compiler_params=pltpu.CompilerParams(vmem_limit_bytes=limit),
+        cost_estimate=cost,
+    )(*args)
+
+
+def dot(a, b):
+    return jnp.dot(a, b, preferred_element_type=f32)
+
+
+def onehot(shape, want):
+    row = lax.broadcasted_iota(jnp.int32, shape, 0)
+    col = lax.broadcasted_iota(jnp.int32, shape, 1)
+    return want(row, col).astype(f32).astype(bf16)
+
+
+def attend_body(picks, lengths, queries, cache, w_uv, out, wide):
+    rows, heads, _ = queries.shape
+    latent_width = w_uv.shape[1]
+    vdim = w_uv.shape[2]
+    for r in range(rows):
+        keys = cache[r]
+        scores = (
+            lax.dot_general(queries[r], keys, (((1,), (1,)), ((), ())), preferred_element_type=f32)
+            * score_scale
+        )
+        live = lax.broadcasted_iota(jnp.int32, scores.shape, 1) < lengths[r]
+        scores = jnp.where(live, scores, -1e30)
+        top = jnp.max(scores, axis=-1, keepdims=True)
+        raw = jnp.where(live, jnp.exp(scores - top), 0.0)
+        probs = (raw / jnp.sum(raw, axis=-1, keepdims=True)).astype(bf16)
+        wide[r] = dot(probs, keys[:, :latent_width])
+    copies = out.shape[0]
+    per = out.shape[2] // vdim
+    for h in range(heads):
+        value = dot(wide[:, h, :].astype(bf16), w_uv[h]).astype(bf16)
+        piece, lane = h // per, (h % per) * vdim
+        for e in range(copies):
+            out[e, piece * rows : (piece + 1) * rows, lane : lane + vdim] = value
+
+
+def plan_body(picks):
+    core = lax.axis_index("tp") % 2
+    _, lines, packed_lines = picks.shape
+    ep = lax.axis_size("ep")
+    rows = lines // ep
+    for half in range(2):
+
+        def want(row, col):
+            block = row // rows
+            parity = jnp.where(block < ep // 2, core, 1 - core)
+            source = 2 * (block % (ep // 2)) + parity
+            return col == source * 2 * rows + half * rows + row % rows
+
+        picks[half] = onehot((lines, packed_lines), want)
+
+
+def project_body(values, picks, w_out, keep, send):
+    ep, packed, width = values.shape
+    rows = packed // 2
+    flat = values[...].reshape(ep * packed, width)
+    total = None
+    for half in range(2):
+        picked = dot(picks[half], flat).astype(bf16)
+        part = dot(picked, w_out[half * width : (half + 1) * width, :])
+        total = part if total is None else total + part
+    for i in range(ep // 2):
+        keep[i] = total[i * rows : (i + 1) * rows]
+        send[i] = total[(i + ep // 2) * rows : (i + ep // 2 + 1) * rows]
+
+
+def pair_body(keep, got, first, second):
+    y = lax.axis_index("tp") // 2
+    first[...] = keep[y] + got[y]
+    second[...] = keep[1 - y] + got[1 - y]
+
+
+def route_body(ids, weights, place, mix):
+    rows, top = ids.shape
+    slots = []
+    for r in range(rows):
+        for k in range(top):
+            expert = ids[r, k]
+            rank = jnp.int32(0)
+            for q in range(r):
+                for j in range(top):
+                    rank = rank + (ids[q, j] == expert).astype(jnp.int32)
+            slots.append((r, k, expert * CAP + rank))
+    packed = place.shape[1]
+    per = packed // 2
+    row = lax.broadcasted_iota(jnp.int32, place.shape, 0)
+    col = lax.broadcasted_iota(jnp.int32, place.shape, 1)
+    slot = (row // packed) * per + row % per
+    half = (row % packed) // per
+    acc = jnp.zeros(place.shape, f32)
+    for r, k, where in slots:
+        acc = acc + jnp.where((slot == where) & (col == half * rows + r), 1.0, 0.0)
+    place[...] = acc.astype(bf16)
+    row = lax.broadcasted_iota(jnp.int32, mix.shape, 0)
+    col = lax.broadcasted_iota(jnp.int32, mix.shape, 1)
+    slot = (col // packed) * per + col % per
+    half = (col % packed) // per
+    acc = jnp.zeros(mix.shape, f32)
+    for r, k, where in slots:
+        acc = acc + jnp.where(
+            (slot == where) & (row // (3 * rows) == half) & (row % rows == r), weights[r, k], 0.0
+        )
+    high = acc.astype(bf16)
+    left = acc - high.astype(f32)
+    middle = left.astype(bf16)
+    low = (left - middle.astype(f32)).astype(bf16)
+    part = (row // rows) % 3
+    mix[...] = jnp.where(
+        part == 0, high.astype(f32), jnp.where(part == 1, middle.astype(f32), low.astype(f32))
+    ).astype(bf16)
+
+
+def spread_body(residual, first, second, place, gain, state, sending, gain_out):
+    gain_out[...] = gain[...]
+    new = (residual[...].astype(f32) + (first[...] + second[...])).astype(bf16)
+    state[...] = new
+    width = new.shape[1] // 2
+    wide = new.astype(f32)
+    halves = jnp.concatenate([wide[:, :width], wide[:, width:]], axis=0).astype(bf16)
+    table = dot(place[...], halves).astype(bf16)
+    sending[...] = table.reshape(sending.shape)
+
+
+def pick_rows(arrived, expert):
+    groups, packed, width = arrived.shape
+    per = packed // 2
+    flat = arrived[...].reshape(groups * packed, width)
+    out = []
+    for half in range(2):
+        want = lambda row, col: (
+            col == (row // CAP) * packed + half * per + expert * CAP + row % CAP
+        )
+        out.append(dot(onehot((groups * CAP, groups * packed), want), flat))
+    return jnp.concatenate(out, axis=1)
+
+
+def expert_partial(arrived, gain, w_gate, w_up, expert, store):
+    rows = pick_rows(arrived, expert)
+    square = jnp.sum(rows * rows, axis=1, keepdims=True)
+    scaled = (rows * gain[...]).astype(bf16)
+    hid = w_gate.shape[2]
+    for p in range(HSPLIT):
+        at = expert * HSPLIT + p
+        store(p * hid, dot(scaled, w_gate[at]))
+        store((HSPLIT + p) * hid, dot(scaled, w_up[at]))
+    high = square.astype(bf16).astype(f32)
+    middle = (square - high).astype(bf16).astype(f32)
+    low = square - high - middle
+    lane = lax.broadcasted_iota(jnp.int32, (rows.shape[0], 128), 1)
+    store(
+        2 * HSPLIT * hid,
+        jnp.where(
+            lane == 0,
+            high,
+            jnp.where(lane == 1, middle, jnp.where(lane == 2, low, 0.0)),
+        ),
+    )
+
+
+def experts_away_body(arrived, gain, w_gate, w_up, out):
+    core = lax.axis_index("tp") % 2
+
+    def store(lane, value):
+        out[:, lane : lane + value.shape[1]] = value.astype(bf16)
+
+    expert_partial(arrived, gain, w_gate, w_up, 1 - core, store)
+
+
+def experts_own_body(arrived, gain, w_gate, w_up, out):
+    core = lax.axis_index("tp") % 2
+
+    def store(lane, value):
+        out[:, lane : lane + value.shape[1]] = value
+
+    expert_partial(arrived, gain, w_gate, w_up, core, store)
+
+
+def merge_body(own, got, total, send):
+    whole = own[...] + got[...].astype(f32)
+    total[...] = whole
+    tail = whole.shape[1] - 128
+    send[:, :tail] = whole[:, :tail].astype(bf16)
+    square = jnp.sum(whole[:, tail:], axis=1, keepdims=True)
+    high = square.astype(bf16).astype(f32)
+    middle = (square - high).astype(bf16).astype(f32)
+    low = square - high - middle
+    lane = lax.broadcasted_iota(jnp.int32, (whole.shape[0], 128), 1)
+    send[:, tail:] = jnp.where(
+        lane == 0,
+        high,
+        jnp.where(lane == 1, middle, jnp.where(lane == 2, low, 0.0)),
+    ).astype(bf16)
+
+
+def act_body(total, got, out):
+    hidden = out.shape[1]
+    whole = total[...] + got[...].astype(f32)
+    square = jnp.sum(whole[:, 2 * hidden :], axis=1, keepdims=True)
+    inv_rms = lax.rsqrt(square / D + norm_eps)
+    gate = whole[:, :hidden] * inv_rms
+    up = whole[:, hidden : 2 * hidden] * inv_rms
+    out[...] = (gate / (1.0 + jnp.exp(-gate)) * up).astype(bf16)
+
+
+def down_one(act, w_down, expert):
+    hid = w_down.shape[1]
+    total = None
+    for p in range(HSPLIT):
+        part = dot(act[:, p * hid : (p + 1) * hid], w_down[expert * HSPLIT + p])
+        total = part if total is None else total + part
+    return total.astype(bf16)
+
+
+def down_body(act, act_away, w_down, out):
+    core = lax.axis_index("tp") % 2
+    groups, packed, width = out.shape
+    per = packed // 2
+    table = None
+    for expert, source in ((core, act), (1 - core, act_away)):
+        block = down_one(source, w_down, expert)
+        for half in range(2):
+            want = lambda row, col: (
+                row == (col // CAP) * packed + half * per + expert * CAP + col % CAP
+            )
+            part = dot(
+                onehot((groups * packed, groups * CAP), want),
+                block[:, half * width : (half + 1) * width],
+            )
+            table = part if table is None else table + part
+    out[...] = table.astype(bf16).reshape(out.shape)
+
+
+def finish_body(state, back, mix, out):
+    groups, packed, width = back.shape
+    rows = state.shape[0]
+    mixed = dot(mix[...], back[...].reshape(groups * packed, width))
+    for half in range(2):
+        base = half * 3 * rows
+        add = (
+            mixed[base : base + rows]
+            + mixed[base + rows : base + 2 * rows]
+            + mixed[base + 2 * rows : base + 3 * rows]
+        )
+        lanes = slice(half * width, (half + 1) * width)
+        out[:, lanes] = (state[:, lanes].astype(f32) + add).astype(bf16)
+
 
 def local(
+    queries,
+    cache,
+    lengths,
+    w_uv,
+    w_out,
+    residual,
+    gain,
+    expert_ids,
+    expert_weights,
+    w_gate,
+    w_up,
+    w_down,
+):
+    sec, ep, tp = (lax.axis_size(a) for a in ("sec", "ep", "tp"))
+    rows, heads, _ = queries.shape
+    columns = residual.shape[1]
+    vdim = w_uv.shape[2]
+    groups = sec * ep
+    slots = EXPERTS // groups * CAP
+    half = columns // 2
+    hidden = HSPLIT * w_gate.shape[2]
+    lines = groups * CAP
+    swap_core = [(t, t ^ 1) for t in range(tp)]
+    swap_chip = [(t, t ^ 2) for t in range(tp)]
+
+    place, mix = call(
+        route_body,
+        [((groups * 2 * slots, 2 * rows), bf16), ((6 * rows, groups * 2 * slots), bf16)],
+        (expert_ids, expert_weights),
+        [SMEM, SMEM],
+    )
+    (picks,) = call(
+        plan_body, [((2, ep * rows, 2 * ep * rows), bf16)], (), [], cost=COST0
+    )
+    (values,) = call(
+        attend_body,
+        [((ep, 2 * rows, heads * vdim // 2), bf16)],
+        (picks, lengths, queries, cache, w_uv),
+        [VMEM, SMEM, VMEM, VMEM, VMEM],
+        [pltpu.VMEM((rows, heads, w_uv.shape[1]), f32)],
+        cost=COST1,
+    )
+    values = lax.all_to_all(values, "ep", split_axis=0, concat_axis=0, tiled=True)
+    keep, send = call(
+        project_body,
+        [((ep // 2, rows, columns), f32)] * 2,
+        (values, picks, w_out),
+        [VMEM, VMEM, VMEM],
+        cost=COST2,
+    )
+    got = lax.ppermute(send, "tp", swap_core)
+    first, second = call(
+        pair_body, [((rows, columns), f32)] * 2, (keep, got), [VMEM, VMEM]
+    )
+
+    def turn(flip):
+        pairs = []
+        for s in range(sec):
+            for e in range(ep):
+                for t in range(tp):
+                    to = (s * ep + t % 2 + 2 * ((t // 2) ^ flip)) * tp + e
+                    pairs.append(((s * ep + e) * tp + t, to))
+        return pairs
+
+    axes = ("sec", "ep", "tp")
+    first = lax.ppermute(first, axes, turn(0))
+    second = lax.ppermute(second, axes, turn(1))
+    state, sending, gain = call(
+        spread_body,
+        [((rows, columns), bf16), ((groups, 2 * slots, half), bf16), ((1, columns), f32)],
+        (residual, first, second, place, gain.reshape(1, columns)),
+        [VMEM] * 5,
+        cost=cost(20),
+    )
+    arrived = lax.all_to_all(sending, ("sec", "ep"), split_axis=0, concat_axis=0, tiled=True)
+    wide = 2 * hidden + 128
+    (away,) = call(
+        experts_away_body,
+        [((lines, wide), bf16)],
+        (arrived, gain, w_gate, w_up),
+        [VMEM] * 4,
+        cost=cost(20),
+    )
+    away = lax.ppermute(away, "tp", swap_core)
+    (own,) = call(
+        experts_own_body,
+        [((lines, wide), f32)],
+        (arrived, gain, w_gate, w_up),
+        [VMEM] * 4,
+        cost=cost(20),
+    )
+    total, send = call(
+        merge_body, [((lines, wide), f32), ((lines, wide), bf16)], (own, away), [VMEM] * 2
+    )
+    got = lax.ppermute(send, "tp", swap_chip)
+    (act,) = call(act_body, [((lines, hidden), bf16)], (total, got), [VMEM] * 2)
+    act_away = lax.ppermute(act, "tp", swap_core)
+    (back,) = call(
+        down_body,
+        [((groups, 2 * slots, half), bf16)],
+        (act, act_away, w_down),
+        [VMEM] * 3,
+    )
+    back = lax.all_to_all(back, ("sec", "ep"), split_axis=0, concat_axis=0, tiled=True)
+    (out,) = call(finish_body, [((rows, columns), bf16)], (state, back, mix), [VMEM] * 3)
+    return out
+
+
+def local_any(
     queries,
     cache,
     lengths,
@@ -113,4 +494,7 @@
         P(("sec", "ep"), None, "tp"),
     )
     out_specs = P(("sec", "ep"), "tp")
-    return jax.shard_map(local, mesh=mesh, in_specs=in_specs, out_specs=out_specs, check_vma=False)
+    shape = mesh.shape
+    small = shape["ep"] == 4 and shape["tp"] == 4 and shape["sec"] == 2
+    body = local if small else local_any
+    return jax.shard_map(body, mesh=mesh, in_specs=in_specs, out_specs=out_specs, check_vma=False)

time: 213 us -> 66.9 us (0.31)
  waiting for transfers between devices: 91.9 us -> 9.28 us
  matrix products: 30.3 us -> 0 us
  blocking collectives: 50.2 us -> 35.8 us
  Pallas kernels: 0 us -> 13.4 us
  between operations: 13.6 us -> 0.3 us
  local copies, waits for them, and re-layouts: 11.2 us -> 1.66 us
  other arithmetic: 4.42 us -> 0.01 us
  starting transfers between devices: 10.3 us -> 6.25 us
    unnamed x3 -> x0, waiting for transfers between devices: 40 us -> none
    dot_general x7 -> x0, matrix products: 30.3 us -> none  [the longest x1 7.95 us: local(): jnp.einsum('gpcd,pdh->gpch', scaled, w_gate, preferred_element_type=jnp.f...]
    all_to_all x2 -> x0, waiting for transfers between devices: 28.5 us -> none  [the longest x1 22.9 us: local(): lax.all_to_all(piece_out.reshape(groups, local_pieces * CAP, column_count...]
    psum x1 -> x0, waiting for transfers between devices: 23.3 us -> none  [local(): gate_part, up_part, squares = lax.psum((gate_part, up_part, squares), 'tp')]
    all_to_all x0 -> x2, blocking collectives: none -> 21.7 us  [the longest x1 11.9 us: local(): lax.all_to_all(values, 'ep', split_axis=0, concat_axis=0, tiled=True)]
    all_to_all x1, blocking collectives: 29.1 us -> 14 us  [local(): lax.all_to_all(sending, ('sec', 'ep'), split_axis=0, concat_axis=0, tiled...]
    all_gather x1 -> x0, blocking collectives: 14.9 us -> none  [local(): lax.all_gather(values, 'ep', axis=0, tiled=True)]
    pallas_call x0 -> x12, Pallas kernels: none -> 13.4 us  [call(): pl.pallas_call(body, out_shape=[jax.ShapeDtypeStruct(s, d) for s, d in ou...]
  transfers between devices with their start and end apart: 4 -> 6, of which waited for: 4 -> 4; matrix products, arithmetic and copies ran while one was open for 0% -> 0% of each run, Pallas kernels for 0% -> 4%
where the time goes in v1:
time: 66.9 us; the launch traced here: 66.7 us
  blocking collectives  35.8 us (54%)
  Pallas kernels  13.4 us (20%)
  waiting for transfers between devices  9.28 us (14%)
  starting transfers between devices  6.25 us (9%)
  local copies, waits for them, and re-layouts  1.66 us (2%)
    all_to_all x1, blocking collectives, local(): lax.all_to_all(sending, ('sec', 'ep'), split_axis=0, concat_axis=0, tiled...  14 us
    pallas_call x12, Pallas kernels, call(): pl.pallas_call(body, out_shape=[jax.ShapeDtypeStruct(s, d) for s, d in ou...  13.4 us
    all_to_all x1, blocking collectives, local(): lax.all_to_all(values, 'ep', split_axis=0, concat_axis=0, tiled=True)  11.9 us
    all_to_all x1, blocking collectives, local(): lax.all_to_all(back, ('sec', 'ep'), split_axis=0, concat_axis=0, tiled=True)  9.88 us
    ppermute x1, waiting for transfers between devices, local(): got = lax.ppermute(send, 'tp', swap_chip)  5.97 us
    ppermute x1, starting transfers between devices, local(): second = lax.ppermute(second, axes, turn(1))  5.31 us
    unnamed x44, local copies, waits for them, and re-layouts  1.65 us
  transfers between devices with their start and end apart: 6, of which 4 were waited for; matrix products, arithmetic and copies ran while one was open for 0% of the time, Pallas kernels for 4%

profile of v1, /device:TPU:0, one launch (start us, length us, event | category | flops | bytes accessed | tf_op | source)
XLA Modules:
  0.0 66.7 jit_solution(1547371415138308202)
XLA Ops:
  0.0 1.5 %copy-done.2 = bf16[16,512,128]{2,1,0:T(8,128)(2,1)S(1)} copy-done((bf16[16,512,128]{2,1,0:T(8,128)(2,1)S(1)}, bf16[16,512,128]{2,1,0:T(8,128)(2,1)}, u32[]{:S(2)}) %copy-start.2) | copy-done | bytes 2097176
  1.6 0.0 copy-done.6
  1.6 0.0 copy-done.3
  1.6 0.0 copy-done.4
  1.6 2.3 %shard_map.119 = bf16[4,8,1024]{2,1,0:T(8,128)(2,1)S(1)} custom-call(bf16[2,16,32]{2,1,0:T(8,128)(2,1)S(1)} %shard_map.118.picks, s32[4]{0:T(128)S(1)} %copy-done.6, bf16[4,16,576]{2,1,0:T(8,128)(2,1)S(1)} %copy-done.4, bf16[4,32,576]{2,1,0:T(8,128)(2,1)S(1)} %copy-done.3, bf16[16,512,128]{2,1,0:T(8,128)(2,1)S(1)} %copy-done.2), custom_call_target="tpu_custom_call" | custom-call | flops 30000001024 | bytes 1000000 | tf_op jit(solution)/shard_map/pallas_call | solution.py:31
  3.9 11.9 %all_to_all.15.values = bf16[4,8,1024]{2,1,0:T(8,128)(2,1)S(1)} all-to-all(bf16[4,8,1024]{2,1,0:T(8,128)(2,1)S(1)} %shard_map.119), channel_id=1, replica_groups=mesh['sec'=2,'ep'=4,'tp'=4] {'ep'}, dimensions={0} | all-to-all | bytes 131072 | tf_op jit(solution)/shard_map/all_to_all | solution.py:331
  15.8 0.0 slice-done.12
  15.8 0.0 slice-done.13
  15.8 0.0 copy-start
  15.8 0.0 copy-start.1
  15.8 0.0 copy-start.5
  15.8 0.0 slice-start.4
  15.9 0.0 slice-start.5
  15.9 0.0 slice-start.6
  15.9 0.0 slice-start.8
  15.9 0.0 slice-start.9
  15.9 0.0 slice-start.10
  15.9 1.2 %shard_map.120 = (f32[2,4,1792]{2,1,0:T(4,128)S(1)}, f32[2,4,1792]{2,1,0:T(4,128)S(1)}) custom-call(bf16[4,8,1024]{2,1,0:T(8,128)(2,1)S(1)} %all_to_all.15.values, bf16[2,16,32]{2,1,0:T(8,128)(2,1)S(1)} %shard_map.118.picks, bf16[2048,1792]{1,0:T(8,128)(2,1)S(1)} %bitcast.7), custom_call_target="tpu_custom_call" | custom-call | flops 60000002048 | bytes 1000000 | tf_op jit(solution)/shard_map/pallas_call | solution.py:31
  17.1 0.0 collective-permute-start
  17.1 1.2 %collective-permute-done.got = f32[2,4,1792]{2,1,0:T(4,128)S(1)} collective-permute-done((f32[2,4,1792]{2,1,0:T(4,128)S(1)}, f32[2,4,1792]{2,1,0:T(4,128)S(1)}, u32[]{:S(2)}, u32[]{:S(2)}) %collective-permute-start) | collective-permute-done | bytes 57376 | tf_op jit(solution)/shard_map/ppermute | solution.py:339
  18.3 0.8 %collective-permute-start.1 = (f32[4,1792]{1,0:T(4,128)S(1)}, f32[4,1792]{1,0:T(4,128)S(1)}, u32[]{:S(2)}, u32[]{:S(2)}) collective-permute-start(f32[4,1792]{1,0:T(4,128)S(1)} %get-tuple-element.18), channel_id=1, source_target_pairs={{0,0},{1,4},{2,8},{3,12},{4,1},{5,5},{6,9},{7,13},{8,2},{9,6},{10,... | collective-permute-start | bytes 86024 | tf_op jit(solution)/shard_map/ppermute | solution.py:354
  19.1 5.3 %collective-permute-start.2 = (f32[4,1792]{1,0:T(4,128)S(1)}, f32[4,1792]{1,0:T(4,128)S(1)}, u32[]{:S(2)}, u32[]{:S(2)}) collective-permute-start(f32[4,1792]{1,0:T(4,128)S(1)} %get-tuple-element.19), channel_id=1, source_target_pairs={{0,8},{1,12},{2,0},{3,4},{4,9},{5,13},{6,1},{7,5},{8,10},{9,14},{1... | collective-permute-start | bytes 86024 | tf_op jit(solution)/shard_map/ppermute | solution.py:355
  24.5 0.0 copy-done.7
  24.5 0.0 copy-done
  24.5 0.0 copy-done.1
  24.5 0.8 %shard_map.122 = (bf16[64,8]{1,0:T(8,128)(2,1)S(1)}, bf16[24,64]{1,0:T(8,128)(2,1)S(1)}) custom-call(s32[4,4]{1,0:T(4,128)S(1)} %copy-done, f32[4,4]{1,0:T(4,128)S(1)} %copy-done.1), custom_call_target="tpu_custom_call" | custom-call | tf_op jit(solution)/shard_map/pallas_call | solution.py:31
  25.3 0.0 collective-permute-done.1.first
  25.3 0.8 %collective-permute-done.2.second = f32[4,1792]{1,0:T(4,128)S(1)} collective-permute-done((f32[4,1792]{1,0:T(4,128)S(1)}, f32[4,1792]{1,0:T(4,128)S(1)}, u32[]{:S(2)}, u32[]{:S(2)}) %collective-permute-start.2) | collective-permute-done | bytes 28704 | tf_op jit(solution)/shard_map/ppermute | solution.py:355
  26.1 0.0 copy-done.5
  26.1 0.2 shard_map.123
  26.2 14.0 %all_to_all.16.arrived = bf16[8,8,896]{2,1,0:T(8,128)(2,1)S(1)} all-to-all(bf16[8,8,896]{2,1,0:T(8,128)(2,1)S(1)} %get-tuple-element.22), channel_id=1, replica_groups=mesh['sec'=2,'ep'=4,'tp'=4] {'sec','ep'}, dimensions={0} | all-to-all | bytes 229376 | tf_op jit(solution)/shard_map/all_to_all | solution.py:363
  40.3 0.0 slice-done.4
  40.3 0.0 slice-start
  40.4 0.0 slice-start.1
  40.4 2.1 %shard_map.125 = bf16[16,4224]{1,0:T(8,128)(2,1)S(1)} custom-call(bf16[8,8,896]{2,1,0:T(8,128)(2,1)S(1)} %all_to_all.16.arrived, f32[1,1792]{1,0:T(1,128)S(1)} %get-tuple-element.23.gain, bf16[16,1792,256]{2,1,0:T(8,128)(2,1)S(1)} %bitcast.3, bf16[16,1792,256]{2,1,0:T(8,128)(2,1)S(1)} %bitcast.5), custom_call_target="tpu_custom_call" | custom-call | flops 20000000000 | bytes 1000000 | tf_op jit(solution)/shard_map/pallas_call | solution.py:31
  42.5 0.0 collective-permute-start.3
  42.5 2.1 %shard_map.124.own = f32[16,4224]{1,0:T(8,128)S(1)} custom-call(bf16[8,8,896]{2,1,0:T(8,128)(2,1)S(1)} %all_to_all.16.arrived, f32[1,1792]{1,0:T(1,128)S(1)} %get-tuple-element.23.gain, bf16[16,1792,256]{2,1,0:T(8,128)(2,1)S(1)} %bitcast.3, bf16[16,1792,256]{2,1,0:T(8,128)(2,1)S(1)} %bitcast.5), custom_call_target="tpu_custom_call" | custom-call | flops 20000000000 | bytes 1000000 | tf_op jit(solution)/shard_map/pallas_call | solution.py:31
  44.6 0.0 collective-permute-done.3.got
  44.6 0.1 shard_map.126
  44.7 0.0 collective-permute-start.4
  44.8 6.0 %collective-permute-done.4.got = bf16[16,4224]{1,0:T(8,128)(2,1)S(1)} collective-permute-done((bf16[16,4224]{1,0:T(8,128)(2,1)S(1)}, bf16[16,4224]{1,0:T(8,128)(2,1)S(1)}, u32[]{:S(2)}, u32[]{:S(2)}) %collective-permute-start.4) | collective-permute-done | bytes 135200 | tf_op jit(solution)/shard_map/ppermute | solution.py:383
  50.8 0.1 shard_map.127.act
  50.9 0.1 collective-permute-start.5
  51.0 1.2 %collective-permute-done.5.act_away = bf16[16,2048]{1,0:T(8,128)(2,1)S(1)} collective-permute-done((bf16[16,2048]{1,0:T(8,128)(2,1)S(1)}, bf16[16,2048]{1,0:T(8,128)(2,1)S(1)}, u32[]{:S(2)}, u32[]{:S(2)}) %collective-permute-start.5) | collective-permute-done | bytes 65568 | tf_op jit(solution)/shard_map/ppermute | solution.py:385
  52.2 0.0 slice-done.1
  52.2 3.8 %shard_map.128 = bf16[8,8,896]{2,1,0:T(8,128)(2,1)S(1)} custom-call(bf16[16,2048]{1,0:T(8,128)(2,1)S(1)} %shard_map.127.act, bf16[16,2048]{1,0:T(8,128)(2,1)S(1)} %collective-permute-done.5.act_away, bf16[16,256,1792]{2,1,0:T(8,128)(2,1)S(1)} %bitcast.1), custom_call_target="tpu_custom_call" | custom-call | tf_op jit(solution)/shard_map/pallas_call | solution.py:31
  56.0 9.9 %all_to_all.17.back = bf16[8,8,896]{2,1,0:T(8,128)(2,1)S(1)} all-to-all(bf16[8,8,896]{2,1,0:T(8,128)(2,1)S(1)} %shard_map.128), channel_id=1, replica_groups=mesh['sec'=2,'ep'=4,'tp'=4] {'sec','ep'}, dimensions={0} | all-to-all | bytes 229376 | tf_op jit(solution)/shard_map/all_to_all | solution.py:392
  65.9 0.7 %shard_map.129 = bf16[4,1792]{1,0:T(4,128)(2,1)} custom-call(bf16[4,1792]{1,0:T(4,128)(2,1)S(1)} %get-tuple-element.21.state, bf16[8,8,896]{2,1,0:T(8,128)(2,1)S(1)} %all_to_all.17.back, bf16[24,64]{1,0:T(8,128)(2,1)S(1)} %get-tuple-element.26.mix), custom_call_target="tpu_custom_call" | custom-call | tf_op jit(solution)/shard_map/pallas_call | solution.py:31
  (28 shorter events, 0.1 us)
Async XLA Ops:
  0.0 1.6 %copy-start.2 = (bf16[16,512,128]{2,1,0:T(8,128)(2,1)S(1)}, bf16[16,512,128]{2,1,0:T(8,128)(2,1)}, u32[]{:S(2)}) copy-start(bf16[16,512,128]{2,1,0:T(8,128)(2,1)} %w_uv.1) | copy-start | bytes 6291460
  0.0 1.6 %copy-start.6 = (s32[4]{0:T(128)S(1)}, s32[4]{0:T(128)}, u32[]{:S(2)}) copy-start(s32[4]{0:T(128)} %lengths.1) | copy-start | bytes 52
  0.0 1.6 %copy-start.3 = (bf16[4,32,576]{2,1,0:T(8,128)(2,1)S(1)}, bf16[4,32,576]{2,1,0:T(8,128)(2,1)}, u32[]{:S(2)}) copy-start(bf16[4,32,576]{2,1,0:T(8,128)(2,1)} %cache.1) | copy-start | bytes 442372
  0.0 1.6 %copy-start.4 = (bf16[4,16,576]{2,1,0:T(8,128)(2,1)S(1)}, bf16[4,16,576]{2,1,0:T(8,128)(2,1)}, u32[]{:S(2)}) copy-start(bf16[4,16,576]{2,1,0:T(8,128)(2,1)} %queries.1) | copy-start | bytes 221188
  0.0 15.8 %slice-start.12 = ((s8[7340032]{0:T(1024)(128)(4,1)}), s8[4194304]{0:T(1024)(128)(4,1)S(1)}, s32[]{:S(2)}) async-start(s8[7340032]{0:T(1024)(128)(4,1)} %bitcast.6), calls=%async_computation.15 | async-start | bytes 8388608
  1.6 14.2 %slice-start.13 = ((s8[7340032]{0:T(1024)(128)(4,1)}), s8[3145728]{0:T(1024)(128)(4,1)S(1)}, s32[]{:S(2)}) async-start(s8[7340032]{0:T(1024)(128)(4,1)} %bitcast.6), calls=%async_computation.16 | async-start | bytes 6291456
  15.8 8.7 %copy-start.7 = (f32[1792]{0:T(1024)S(1)}, f32[1792]{0:T(1024)}, u32[]{:S(2)}) copy-start(f32[1792]{0:T(1024)} %param.18) | copy-start | bytes 21508
  15.8 8.7 %copy-start = (s32[4,4]{1,0:T(4,128)S(1)}, s32[4,4]{1,0:T(4,128)}, u32[]{:S(2)}) copy-start(s32[4,4]{1,0:T(4,128)} %ids.1) | copy-start | bytes 196
  15.8 8.7 %copy-start.1 = (f32[4,4]{1,0:T(4,128)S(1)}, f32[4,4]{1,0:T(4,128)}, u32[]{:S(2)}) copy-start(f32[4,4]{1,0:T(4,128)} %weights.1) | copy-start | bytes 196
  15.8 10.2 %copy-start.5 = (bf16[4,1792]{1,0:T(4,128)(2,1)S(1)}, bf16[4,1792]{1,0:T(4,128)(2,1)}, u32[]{:S(2)}) copy-start(bf16[4,1792]{1,0:T(4,128)(2,1)} %residual.1) | copy-start | bytes 43012
  15.8 24.4 %slice-start.4 = ((s8[14680064]{0:T(1024)(128)(4,1)}), s8[4194304]{0:T(1024)(128)(4,1)S(1)}, s32[]{:S(2)}) async-start(s8[14680064]{0:T(1024)(128)(4,1)} %bitcast.2), calls=%async_computation.7 | async-start | bytes 8388608
  15.9 24.4 %slice-start.5 = ((s8[14680064]{0:T(1024)(128)(4,1)}), s8[4194304]{0:T(1024)(128)(4,1)S(1)}, s32[]{:S(2)}) async-start(s8[14680064]{0:T(1024)(128)(4,1)} %bitcast.2), calls=%async_computation.8 | async-start | bytes 8388608
  15.9 24.4 %slice-start.6 = ((s8[14680064]{0:T(1024)(128)(4,1)}), s8[4194304]{0:T(1024)(128)(4,1)S(1)}, s32[]{:S(2)}) async-start(s8[14680064]{0:T(1024)(128)(4,1)} %bitcast.2), calls=%async_computation.9 | async-start | bytes 8388608
  15.9 24.4 %slice-start.8 = ((s8[14680064]{0:T(1024)(128)(4,1)}), s8[2097152]{0:T(1024)(128)(4,1)S(1)}, s32[]{:S(2)}) async-start(s8[14680064]{0:T(1024)(128)(4,1)} %bitcast.4), calls=%async_computation.11 | async-start | bytes 4194304
  15.9 24.4 %slice-start.9 = ((s8[14680064]{0:T(1024)(128)(4,1)}), s8[4194304]{0:T(1024)(128)(4,1)S(1)}, s32[]{:S(2)}) async-start(s8[14680064]{0:T(1024)(128)(4,1)} %bitcast.4), calls=%async_computation.12 | async-start | bytes 8388608
  15.9 24.4 %slice-start.10 = ((s8[14680064]{0:T(1024)(128)(4,1)}), s8[4194304]{0:T(1024)(128)(4,1)S(1)}, s32[]{:S(2)}) async-start(s8[14680064]{0:T(1024)(128)(4,1)} %bitcast.4), calls=%async_computation.13 | async-start | bytes 8388608
  17.1 1.3 %collective-permute-start = (f32[2,4,1792]{2,1,0:T(4,128)S(1)}, f32[2,4,1792]{2,1,0:T(4,128)S(1)}, u32[]{:S(2)}, u32[]{:S(2)}) collective-permute-start(f32[2,4,1792]{2,1,0:T(4,128)S(1)} %get-tuple-element.17), channel_id=1, source_target_pairs={{0,1},{1,0},{2,3},{3,2},{4,5},{5,4},{6,7},{7,6},{8,9},{9,8},{10,11... | collective-permute-start | bytes 172040 | tf_op jit(solution)/shard_map/ppermute | solution.py:339
  18.3 6.9 %collective-permute-start.1 = (f32[4,1792]{1,0:T(4,128)S(1)}, f32[4,1792]{1,0:T(4,128)S(1)}, u32[]{:S(2)}, u32[]{:S(2)}) collective-permute-start(f32[4,1792]{1,0:T(4,128)S(1)} %get-tuple-element.18), channel_id=1, source_target_pairs={{0,0},{1,4},{2,8},{3,12},{4,1},{5,5},{6,9},{7,13},{8,2},{9,6},{10,... | collective-permute-start | bytes 86024 | tf_op jit(solution)/shard_map/ppermute | solution.py:354
  19.1 6.9 %collective-permute-start.2 = (f32[4,1792]{1,0:T(4,128)S(1)}, f32[4,1792]{1,0:T(4,128)S(1)}, u32[]{:S(2)}, u32[]{:S(2)}) collective-permute-start(f32[4,1792]{1,0:T(4,128)S(1)} %get-tuple-element.19), channel_id=1, source_target_pairs={{0,8},{1,12},{2,0},{3,4},{4,9},{5,13},{6,1},{7,5},{8,10},{9,14},{1... | collective-permute-start | bytes 86024 | tf_op jit(solution)/shard_map/ppermute | solution.py:355
  26.1 14.2 %slice-start.7 = ((s8[14680064]{0:T(1024)(128)(4,1)}), s8[2097152]{0:T(1024)(128)(4,1)S(1)}, s32[]{:S(2)}) async-start(s8[14680064]{0:T(1024)(128)(4,1)} %bitcast.2), calls=%async_computation.10 | async-start | bytes 4194304
  26.1 14.2 %slice-start.11 = ((s8[14680064]{0:T(1024)(128)(4,1)}), s8[4194304]{0:T(1024)(128)(4,1)S(1)}, s32[]{:S(2)}) async-start(s8[14680064]{0:T(1024)(128)(4,1)} %bitcast.4), calls=%async_computation.14 | async-start | bytes 8388608
  40.3 11.9 %slice-start = ((s8[14680064]{0:T(1024)(128)(4,1)}), s8[4194304]{0:T(1024)(128)(4,1)S(1)}, s32[]{:S(2)}) async-start(s8[14680064]{0:T(1024)(128)(4,1)} %bitcast), calls=%async_computation.3 | async-start | bytes 8388608
  40.4 11.9 %slice-start.1 = ((s8[14680064]{0:T(1024)(128)(4,1)}), s8[4194304]{0:T(1024)(128)(4,1)S(1)}, s32[]{:S(2)}) async-start(s8[14680064]{0:T(1024)(128)(4,1)} %bitcast), calls=%async_computation.4 | async-start | bytes 8388608
  42.5 9.7 %slice-start.2 = ((s8[14680064]{0:T(1024)(128)(4,1)}), s8[4194304]{0:T(1024)(128)(4,1)S(1)}, s32[]{:S(2)}) async-start(s8[14680064]{0:T(1024)(128)(4,1)} %bitcast), calls=%async_computation.5 | async-start | bytes 8388608
  42.5 9.7 %slice-start.3 = ((s8[14680064]{0:T(1024)(128)(4,1)}), s8[2097152]{0:T(1024)(128)(4,1)S(1)}, s32[]{:S(2)}) async-start(s8[14680064]{0:T(1024)(128)(4,1)} %bitcast), calls=%async_computation.6 | async-start | bytes 4194304
  42.5 2.2 %collective-permute-start.3 = (bf16[16,4224]{1,0:T(8,128)(2,1)S(1)}, bf16[16,4224]{1,0:T(8,128)(2,1)S(1)}, u32[]{:S(2)}, u32[]{:S(2)}) collective-permute-start(bf16[16,4224]{1,0:T(8,128)(2,1)S(1)} %shard_map.125), channel_id=1, source_target_pairs={{0,1},{1,0},{2,3},{3,2},{4,5},{5,4},{6,7},{7,6},{8,9},{9,8},{10,11... | collective-permute-start | bytes 405512 | tf_op jit(solution)/shard_map/ppermute | solution.py:372
  44.7 6.0 %collective-permute-start.4 = (bf16[16,4224]{1,0:T(8,128)(2,1)S(1)}, bf16[16,4224]{1,0:T(8,128)(2,1)S(1)}, u32[]{:S(2)}, u32[]{:S(2)}) collective-permute-start(bf16[16,4224]{1,0:T(8,128)(2,1)S(1)} %get-tuple-element.25), channel_id=1, source_target_pairs={{0,2},{1,3},{2,0},{3,1},{4,6},{5,7},{6,4},{7,5},{8,10},{9,11},{10,... | collective-permute-start | bytes 405512 | tf_op jit(solution)/shard_map/ppermute | solution.py:383
  50.9 1.3 %collective-permute-start.5 = (bf16[16,2048]{1,0:T(8,128)(2,1)S(1)}, bf16[16,2048]{1,0:T(8,128)(2,1)S(1)}, u32[]{:S(2)}, u32[]{:S(2)}) collective-permute-start(bf16[16,2048]{1,0:T(8,128)(2,1)S(1)} %shard_map.127.act), channel_id=1, source_target_pairs={{0,1},{1,0},{2,3},{3,2},{4,5},{5,4},{6,7},{7,6},{8,9},{9,8},{10,11... | collective-permute-start | bytes 196616 | tf_op jit(solution)/shard_map/ppermute | solution.py:385

commit v2 on v1

--- a/solution.py
+++ b/solution.py
@@ -24,7 +24,7 @@
     return pl.CostEstimate(flops=micros * 1_000_000_000, bytes_accessed=1_000_000, transcendentals=0)
 
 
-COST0, COST1, COST2 = cost(10), cost(30), cost(60)
+COSTS = [cost(m) for m in (20, 1, 20, 60, 1, 1, 20, 20)]
 
 
 def call(body, outs, args, specs, scratch=(), limit=4 << 20, cost=None):
@@ -49,68 +49,128 @@
     return want(row, col).astype(f32).astype(bf16)
 
 
-def attend_body(picks, lengths, queries, cache, w_uv, out, wide):
+def start_body(pick):
+    me = lax.axis_index("ep")
+    lines = pick.shape[0]
+    block = lines // 4
+    rows = block // 4
+
+    def want(row, col):
+        kind, e, r = row // block, (row % block) // rows, row % rows
+        return col == (e ^ me) * block + kind * rows + r
+
+    pick[...] = onehot(pick.shape, want)
+
+
+def latent_body(lengths, queries, cache, pick, latent):
     rows, heads, _ = queries.shape
-    latent_width = w_uv.shape[1]
-    vdim = w_uv.shape[2]
+    width = latent.shape[2]
+    scores = jnp.concatenate(
+        [
+            lax.dot_general(
+                queries[r], cache[r], (((1,), (1,)), ((), ())), preferred_element_type=f32
+            )
+            for r in range(rows)
+        ],
+        axis=0,
+    )
+    owner = lax.broadcasted_iota(jnp.int32, scores.shape, 0) // heads
+    limit = jnp.full(scores.shape, lengths[0], jnp.int32)
+    for r in range(1, rows):
+        limit = jnp.where(owner == r, lengths[r], limit)
+    live = lax.broadcasted_iota(jnp.int32, scores.shape, 1) < limit
+    scores = jnp.where(live, scores * score_scale, -1e30)
+    top = jnp.max(scores, axis=-1, keepdims=True)
+    raw = jnp.where(live, jnp.exp(scores - top), 0.0)
+    probs = (raw / jnp.sum(raw, axis=-1, keepdims=True)).astype(bf16)
     for r in range(rows):
-        keys = cache[r]
-        scores = (
-            lax.dot_general(queries[r], keys, (((1,), (1,)), ((), ())), preferred_element_type=f32)
-            * score_scale
-        )
-        live = lax.broadcasted_iota(jnp.int32, scores.shape, 1) < lengths[r]
-        scores = jnp.where(live, scores, -1e30)
-        top = jnp.max(scores, axis=-1, keepdims=True)
-        raw = jnp.where(live, jnp.exp(scores - top), 0.0)
-        probs = (raw / jnp.sum(raw, axis=-1, keepdims=True)).astype(bf16)
-        wide[r] = dot(probs, keys[:, :latent_width])
-    copies = out.shape[0]
-    per = out.shape[2] // vdim
-    for h in range(heads):
-        value = dot(wide[:, h, :].astype(bf16), w_uv[h]).astype(bf16)
-        piece, lane = h // per, (h % per) * vdim
-        for e in range(copies):
-            out[e, piece * rows : (piece + 1) * rows, lane : lane + vdim] = value
-
-
-def plan_body(picks):
-    core = lax.axis_index("tp") % 2
-    _, lines, packed_lines = picks.shape
-    ep = lax.axis_size("ep")
-    rows = lines // ep
-    for half in range(2):
-
-        def want(row, col):
-            block = row // rows
-            parity = jnp.where(block < ep // 2, core, 1 - core)
-            source = 2 * (block % (ep // 2)) + parity
-            return col == source * 2 * rows + half * rows + row % rows
-
-        picks[half] = onehot((lines, packed_lines), want)
-
-
-def project_body(values, picks, w_out, keep, send):
-    ep, packed, width = values.shape
-    rows = packed // 2
-    flat = values[...].reshape(ep * packed, width)
-    total = None
-    for half in range(2):
-        picked = dot(picks[half], flat).astype(bf16)
-        part = dot(picked, w_out[half * width : (half + 1) * width, :])
-        total = part if total is None else total + part
-    for i in range(ep // 2):
-        keep[i] = total[i * rows : (i + 1) * rows]
-        send[i] = total[(i + ep // 2) * rows : (i + ep // 2 + 1) * rows]
-
-
-def pair_body(keep, got, first, second):
-    y = lax.axis_index("tp") // 2
-    first[...] = keep[y] + got[y]
-    second[...] = keep[1 - y] + got[1 - y]
-
-
-def route_body(ids, weights, place, mix):
+        latent[r] = dot(probs[r * heads : (r + 1) * heads], cache[r, :, :width])
+
+
+def values_body(ids, latent, w_uv, residual, out):
+    rows, heads, _ = latent.shape
+    per = heads // 2
+    halves = []
+    for piece in range(2):
+        parts = [
+            dot(latent[:, h, :].astype(bf16), w_uv[h]) for h in range(piece * per, (piece + 1) * per)
+        ]
+        halves.append(jnp.concatenate(parts, axis=1))
+    packed = 2 * rows
+    out[:packed] = jnp.concatenate(halves, axis=0).astype(bf16)
+    span = residual.shape[1] // 2
+    wide = residual[...].astype(f32)
+    row = lax.broadcasted_iota(jnp.int32, (rows, 128), 0)
+    lane = lax.broadcasted_iota(jnp.int32, (rows, 128), 1)
+    named = jnp.zeros((rows, 128), f32)
+    for r in range(rows):
+        for k in range(ids.shape[1]):
+            named = jnp.where((row == r) & (lane == k), ids[r, k].astype(f32), named)
+    halves = [
+        jnp.concatenate([wide[:, h * span : (h + 1) * span], named], axis=1) for h in range(2)
+    ]
+    out[packed:] = jnp.concatenate(halves, axis=0).astype(bf16)
+
+
+def project_body(pick, own, got1, got2, got3, w_out, out, extra):
+    packed = own.shape[0] // 2
+    flat = jnp.concatenate([ref[...] for ref in (own, got1, got2, got3)], axis=0)
+    block, width = out.shape[0], own.shape[1]
+    table = dot(pick[...], flat).astype(bf16)
+    out[...] = dot(table[:block], w_out[:width]) + dot(table[block : 2 * block], w_out[width:])
+    extra[...] = table[2 * block :]
+
+
+def add_body(one, two, out):
+    out[...] = (one[...].astype(f32) + two[...].astype(f32)).astype(bf16)
+
+
+def choose_body(extra, got, known, choice):
+    me, sec = lax.axis_index("ep"), lax.axis_index("sec")
+    block = extra.shape[0] // 2
+    rows = block // 4
+    tokens = 2 * block
+    span = known.shape[1] // 2
+    first = jnp.concatenate([extra[:block], got[:block]], axis=0)
+    second = jnp.concatenate([extra[block:], got[block:]], axis=0)
+    known[:, :span] = first[:, :span].astype(f32)
+    known[:, span:] = second[:, :span].astype(f32)
+    ids = first[:, span:].astype(f32)
+    lane = lax.broadcasted_iota(jnp.int32, ids.shape, 1)
+    hits = jnp.zeros(ids.shape, f32)
+    local_experts = EXPERTS // (2 * 4)
+    for x in range(local_experts):
+        expert = ((sec * 4 + me) * local_experts + x).astype(f32)
+        found = jnp.sum(jnp.where((lane < 4) & (ids == expert), 1.0, 0.0), axis=1, keepdims=True)
+        hits = hits + jnp.where(lane == x, found, 0.0)
+    hits = hits.astype(bf16)
+    across = lax.dot_general(
+        onehot((8, 128), lambda row, col: row == col),
+        hits,
+        (((1,), (1,)), ((), ())),
+        preferred_element_type=f32,
+    )
+    earlier = dot(
+        across.astype(bf16),
+        onehot((tokens, tokens), lambda row, col: (row // rows == col // rows) & (row < col)),
+    )
+    slots = 2 * 4 * CAP
+    row = lax.broadcasted_iota(jnp.int32, (slots, tokens), 0)
+    col = lax.broadcasted_iota(jnp.int32, (slots, tokens), 1)
+    group, rank = row // CAP, (row % CAP).astype(f32)
+    same = (group % 4 == (col % block) // rows) & ((group // 4) ^ sec == col // block)
+    for x in range(local_experts):
+        hit = jnp.broadcast_to(across[x : x + 1], (slots, tokens))
+        before = jnp.broadcast_to(earlier[x : x + 1], (slots, tokens))
+        choice[x * slots : (x + 1) * slots] = jnp.where(
+            same & (hit > 0.5) & (before == rank), 1.0, 0.0
+        ).astype(bf16)
+    choice[local_experts * slots :] = onehot(
+        (8, tokens), lambda row, col: (row < rows) & (col == me * rows + row)
+    )
+
+
+def mix_body(ids, weights, mix):
     rows, top = ids.shape
     slots = []
     for r in range(rows):
@@ -121,16 +181,8 @@
                 for j in range(top):
                     rank = rank + (ids[q, j] == expert).astype(jnp.int32)
             slots.append((r, k, expert * CAP + rank))
-    packed = place.shape[1]
+    packed = 8
     per = packed // 2
-    row = lax.broadcasted_iota(jnp.int32, place.shape, 0)
-    col = lax.broadcasted_iota(jnp.int32, place.shape, 1)
-    slot = (row // packed) * per + row % per
-    half = (row % packed) // per
-    acc = jnp.zeros(place.shape, f32)
-    for r, k, where in slots:
-        acc = acc + jnp.where((slot == where) & (col == half * rows + r), 1.0, 0.0)
-    place[...] = acc.astype(bf16)
     row = lax.broadcasted_iota(jnp.int32, mix.shape, 0)
     col = lax.broadcasted_iota(jnp.int32, mix.shape, 1)
     slot = (col // packed) * per + col % per
@@ -150,32 +202,7 @@
     ).astype(bf16)
 
 
-def spread_body(residual, first, second, place, gain, state, sending, gain_out):
-    gain_out[...] = gain[...]
-    new = (residual[...].astype(f32) + (first[...] + second[...])).astype(bf16)
-    state[...] = new
-    width = new.shape[1] // 2
-    wide = new.astype(f32)
-    halves = jnp.concatenate([wide[:, :width], wide[:, width:]], axis=0).astype(bf16)
-    table = dot(place[...], halves).astype(bf16)
-    sending[...] = table.reshape(sending.shape)
-
-
-def pick_rows(arrived, expert):
-    groups, packed, width = arrived.shape
-    per = packed // 2
-    flat = arrived[...].reshape(groups * packed, width)
-    out = []
-    for half in range(2):
-        want = lambda row, col: (
-            col == (row // CAP) * packed + half * per + expert * CAP + row % CAP
-        )
-        out.append(dot(onehot((groups * CAP, groups * packed), want), flat))
-    return jnp.concatenate(out, axis=1)
-
-
-def expert_partial(arrived, gain, w_gate, w_up, expert, store):
-    rows = pick_rows(arrived, expert)
+def expert_partial(rows, gain, w_gate, w_up, expert, store):
     square = jnp.sum(rows * rows, axis=1, keepdims=True)
     scaled = (rows * gain[...]).astype(bf16)
     hid = w_gate.shape[2]
@@ -197,26 +224,40 @@
     )
 
 
-def experts_away_body(arrived, gain, w_gate, w_up, out):
+def experts_away_body(known, same, other, choice, gain, w_gate, w_up, out, mine, state):
     core = lax.axis_index("tp") % 2
-
-    def store(lane, value):
-        out[:, lane : lane + value.shape[1]] = value.astype(bf16)
-
-    expert_partial(arrived, gain, w_gate, w_up, 1 - core, store)
-
-
-def experts_own_body(arrived, gain, w_gate, w_up, out):
-    core = lax.axis_index("tp") % 2
+    block = same.shape[0]
+    lines = out.shape[0]
+    hidden = jnp.concatenate(
+        [
+            (known[:block] + same[...].astype(f32)).astype(bf16),
+            (known[block:] + other[...].astype(f32)).astype(bf16),
+        ],
+        axis=0,
+    )
+    table = dot(choice[...], hidden)
+    first, second = table[:lines], table[lines : 2 * lines]
+    mine[...] = jnp.where(core == 0, first, second).astype(bf16)
+    state[...] = table[2 * lines : 2 * lines + state.shape[0]].astype(bf16)
 
     def store(lane, value):
         out[:, lane : lane + value.shape[1]] = value
 
-    expert_partial(arrived, gain, w_gate, w_up, core, store)
+    rows = jnp.where(core == 0, second, first)
+    expert_partial(rows, gain, w_gate, w_up, 1 - core, store)
+
+
+def experts_own_body(mine, gain, w_gate, w_up, out):
+    core = lax.axis_index("tp") % 2
+
+    def store(lane, value):
+        out[:, lane : lane + value.shape[1]] = value
+
+    expert_partial(mine[...].astype(f32), gain, w_gate, w_up, core, store)
 
 
 def merge_body(own, got, total, send):
-    whole = own[...] + got[...].astype(f32)
+    whole = own[...] + got[...]
     total[...] = whole
     tail = whole.shape[1] - 128
     send[:, :tail] = whole[:, :tail].astype(bf16)
@@ -251,22 +292,30 @@
     return total.astype(bf16)
 
 
-def down_body(act, act_away, w_down, out):
+def scatter_rows(away, own, core, shape):
+    groups, packed, width = shape
+    per = packed // 2
+    lines = groups * CAP
+    both = jnp.concatenate([away, own], axis=0)
+    flat = jnp.concatenate([both[:, :width], both[:, width:]], axis=0)
+
+    def want(row, col):
+        half, block, line = col // (2 * lines), (col // lines) % 2, col % lines
+        expert = jnp.where(block == 0, 1 - core, core)
+        return row == (line // CAP) * packed + half * per + expert * CAP + line % CAP
+
+    return dot(onehot((groups * packed, 4 * lines), want), flat)
+
+
+def down_own_body(act, w_down, out):
     core = lax.axis_index("tp") % 2
-    groups, packed, width = out.shape
-    per = packed // 2
-    table = None
-    for expert, source in ((core, act), (1 - core, act_away)):
-        block = down_one(source, w_down, expert)
-        for half in range(2):
-            want = lambda row, col: (
-                row == (col // CAP) * packed + half * per + expert * CAP + col % CAP
-            )
-            part = dot(
-                onehot((groups * packed, groups * CAP), want),
-                block[:, half * width : (half + 1) * width],
-            )
-            table = part if table is None else table + part
+    out[...] = down_one(act, w_down, core)
+
+
+def down_away_body(act, w_down, done, out):
+    core = lax.axis_index("tp") % 2
+    away = down_one(act, w_down, 1 - core)
+    table = scatter_rows(away, done[...], core, out.shape)
     out[...] = table.astype(bf16).reshape(out.shape)
 
 
@@ -300,93 +349,95 @@
     w_down,
 ):
     sec, ep, tp = (lax.axis_size(a) for a in ("sec", "ep", "tp"))
+    axes = ("sec", "ep", "tp")
     rows, heads, _ = queries.shape
     columns = residual.shape[1]
-    vdim = w_uv.shape[2]
     groups = sec * ep
     slots = EXPERTS // groups * CAP
     half = columns // 2
     hidden = HSPLIT * w_gate.shape[2]
     lines = groups * CAP
-    swap_core = [(t, t ^ 1) for t in range(tp)]
-    swap_chip = [(t, t ^ 2) for t in range(tp)]
-
-    place, mix = call(
-        route_body,
-        [((groups * 2 * slots, 2 * rows), bf16), ((6 * rows, groups * 2 * slots), bf16)],
-        (expert_ids, expert_weights),
-        [SMEM, SMEM],
-    )
-    (picks,) = call(
-        plan_body, [((2, ep * rows, 2 * ep * rows), bf16)], (), [], cost=COST0
+    packed = 2 * rows
+    width = half + 128
+
+    def swap(axis, bit):
+        return [(i, i ^ bit) for i in range(lax.axis_size(axis))]
+
+    def turn(flip):
+        return [
+            ((s * ep + e) * tp + t, ((s ^ flip) * ep + t) * tp + e)
+            for s in range(sec)
+            for e in range(ep)
+            for t in range(tp)
+        ]
+
+    gain = gain.reshape(1, columns)
+    (pick,) = call(start_body, [((4 * ep * rows, 4 * ep * rows), bf16)], (), [], cost=COSTS[0])
+    (latent,) = call(
+        latent_body,
+        [((rows, heads, w_uv.shape[1]), f32)],
+        (lengths, queries, cache, pick),
+        [SMEM, VMEM, VMEM, VMEM],
+        cost=COSTS[1],
     )
     (values,) = call(
-        attend_body,
-        [((ep, 2 * rows, heads * vdim // 2), bf16)],
-        (picks, lengths, queries, cache, w_uv),
-        [VMEM, SMEM, VMEM, VMEM, VMEM],
-        [pltpu.VMEM((rows, heads, w_uv.shape[1]), f32)],
-        cost=COST1,
-    )
-    values = lax.all_to_all(values, "ep", split_axis=0, concat_axis=0, tiled=True)
-    keep, send = call(
+        values_body,
+        [((2 * packed, width), bf16)],
+        (expert_ids, latent, w_uv, residual),
+        [SMEM, VMEM, VMEM, VMEM],
+        cost=COSTS[2],
+    )
+    blocks = [values] + [lax.ppermute(values, "ep", swap("ep", k)) for k in (1, 2, 3)]
+    part, extra = call(
         project_body,
-        [((ep // 2, rows, columns), f32)] * 2,
-        (values, picks, w_out),
-        [VMEM, VMEM, VMEM],
-        cost=COST2,
-    )
-    got = lax.ppermute(send, "tp", swap_core)
-    first, second = call(
-        pair_body, [((rows, columns), f32)] * 2, (keep, got), [VMEM, VMEM]
-    )
-
-    def turn(flip):
-        pairs = []
-        for s in range(sec):
-            for e in range(ep):
-                for t in range(tp):
-                    to = (s * ep + t % 2 + 2 * ((t // 2) ^ flip)) * tp + e
-                    pairs.append(((s * ep + e) * tp + t, to))
-        return pairs
-
-    axes = ("sec", "ep", "tp")
-    first = lax.ppermute(first, axes, turn(0))
-    second = lax.ppermute(second, axes, turn(1))
-    state, sending, gain = call(
-        spread_body,
-        [((rows, columns), bf16), ((groups, 2 * slots, half), bf16), ((1, columns), f32)],
-        (residual, first, second, place, gain.reshape(1, columns)),
-        [VMEM] * 5,
-        cost=cost(20),
-    )
-    arrived = lax.all_to_all(sending, ("sec", "ep"), split_axis=0, concat_axis=0, tiled=True)
+        [((ep * rows, columns), f32), ((2 * ep * rows, width), bf16)],
+        (pick, *blocks, w_out),
+        [VMEM] * 6,
+        cost=COSTS[3],
+    )
+    got = lax.ppermute(part, "tp", swap("tp", 1))
+    beyond = lax.ppermute(extra, "sec", swap("sec", 1))
+    (part,) = call(add_body, [((ep * rows, columns), bf16)], (part, got), [VMEM] * 2, cost=COSTS[4])
+    got = lax.ppermute(part, "tp", swap("tp", 2))
+    (part,) = call(add_body, [((ep * rows, columns), bf16)], (part, got), [VMEM] * 2, cost=COSTS[5])
+    same = lax.ppermute(part, axes, turn(0))
+    cross = lax.ppermute(part, axes, turn(1))
+    known, choice = call(
+        choose_body,
+        [((groups * rows, columns), f32), ((2 * lines + 8, groups * rows), bf16)],
+        (extra, beyond),
+        [VMEM] * 2,
+    )
+    (mix,) = call(
+        mix_body, [((6 * rows, groups * 2 * slots), bf16)], (expert_ids, expert_weights), [SMEM] * 2
+    )
     wide = 2 * hidden + 128
-    (away,) = call(
+    away, mine, state = call(
         experts_away_body,
-        [((lines, wide), bf16)],
-        (arrived, gain, w_gate, w_up),
-        [VMEM] * 4,
-        cost=cost(20),
-    )
-    away = lax.ppermute(away, "tp", swap_core)
+        [((lines, wide), f32), ((lines, columns), bf16), ((rows, columns), bf16)],
+        (known, same, cross, choice, gain, w_gate, w_up),
+        [VMEM] * 7,
+        cost=COSTS[6],
+    )
+    away = lax.ppermute(away, "tp", swap("tp", 1))
     (own,) = call(
         experts_own_body,
         [((lines, wide), f32)],
-        (arrived, gain, w_gate, w_up),
+        (mine, gain, w_gate, w_up),
         [VMEM] * 4,
-        cost=cost(20),
+        cost=COSTS[7],
     )
     total, send = call(
         merge_body, [((lines, wide), f32), ((lines, wide), bf16)], (own, away), [VMEM] * 2
     )
-    got = lax.ppermute(send, "tp", swap_chip)
+    got = lax.ppermute(send, "tp", swap("tp", 2))
     (act,) = call(act_body, [((lines, hidden), bf16)], (total, got), [VMEM] * 2)
-    act_away = lax.ppermute(act, "tp", swap_core)
+    act_away = lax.ppermute(act, "tp", swap("tp", 1))
+    (done,) = call(down_own_body, [((lines, columns), bf16)], (act, w_down), [VMEM] * 2)
     (back,) = call(
-        down_body,
+        down_away_body,
         [((groups, 2 * slots, half), bf16)],
-        (act, act_away, w_down),
+        (act_away, w_down, done),
         [VMEM] * 3,
     )
     back = lax.all_to_all(back, ("sec", "ep"), split_axis=0, concat_axis=0, tiled=True)

time: 66.9 us -> 58.4 us (0.87)
  blocking collectives: 35.8 us -> 0 us
  starting transfers between devices: 6.25 us -> 22.9 us
  waiting for transfers between devices: 9.28 us -> 21.5 us
  Pallas kernels: 13.4 us -> 12.4 us
    all_to_all x3 -> x0, blocking collectives: 35.8 us -> none  [the longest x1 14 us: local(): lax.all_to_all(sending, ('sec', 'ep'), split_axis=0, concat_axis=0, tiled...]
    ppermute x6 -> x11, starting transfers between devices: 6.25 us -> 17.9 us  [the longest x3 5.68 us: local(): lax.ppermute(values, 'ep', swap('ep', k))]
    all_to_all x0 -> x1, waiting for transfers between devices: none -> 6.65 us  [local(): lax.all_to_all(back, ('sec', 'ep'), split_axis=0, concat_axis=0, tiled=True)]
    ppermute x6 -> x11, waiting for transfers between devices: 9.28 us -> 14.9 us  [the longest x3 5.71 us: local(): lax.ppermute(values, 'ep', swap('ep', k))]
    all_to_all x0 -> x1, starting transfers between devices: none -> 5.03 us  [local(): lax.all_to_all(back, ('sec', 'ep'), split_axis=0, concat_axis=0, tiled=True)]
    pallas_call x12 -> x15, Pallas kernels: 13.4 us -> 12.4 us  [call(): pl.pallas_call(body, out_shape=[jax.ShapeDtypeStruct(s, d) for s, d in ou...]
  transfers between devices with their start and end apart: 6 -> 12, of which waited for: 4 -> 8; matrix products, arithmetic and copies ran while one was open for 0% -> 0% of each run, Pallas kernels for 4% -> 7%
where the time goes in v2:
time: 58.4 us; the launch traced here: 58.2 us
  starting transfers between devices  22.9 us (39%)
  waiting for transfers between devices  21.5 us (37%)
  Pallas kernels  12.4 us (21%)
  local copies, waits for them, and re-layouts  1.04 us (2%)
    pallas_call x15, Pallas kernels, call(): pl.pallas_call(body, out_shape=[jax.ShapeDtypeStruct(s, d) for s, d in ou...  12.4 us
    all_to_all x1, waiting for transfers between devices, local(): lax.all_to_all(back, ('sec', 'ep'), split_axis=0, concat_axis=0, tiled=True)  6.65 us
    ppermute x3, waiting for transfers between devices, local(): lax.ppermute(values, 'ep', swap('ep', k))  5.71 us
    ppermute x3, starting transfers between devices, local(): lax.ppermute(values, 'ep', swap('ep', k))  5.68 us
    ppermute x1, starting transfers between devices, local(): got = lax.ppermute(send, 'tp', swap('tp', 2))  5.67 us
    all_to_all x1, starting transfers between devices, local(): lax.all_to_all(back, ('sec', 'ep'), split_axis=0, concat_axis=0, tiled=True)  5.03 us
    ppermute x1, waiting for transfers between devices, local(): got = lax.ppermute(send, 'tp', swap('tp', 2))  4.24 us
    ppermute x1, waiting for transfers between devices, local(): cross = lax.ppermute(part, axes, turn(1))  2.32 us
  transfers between devices with their start and end apart: 12, of which 8 were waited for; matrix products, arithmetic and copies ran while one was open for 0% of the time, Pallas kernels for 7%

profile of v2, /device:TPU:0, one launch (start us, length us, event | category | flops | bytes accessed | tf_op | source)
XLA Modules:
  0.0 58.2 jit_solution(17128103650573272194)
XLA Ops:
  0.1 0.6 %copy-done.6 = s32[4]{0:T(128)S(1)} copy-done((s32[4]{0:T(128)S(1)}, s32[4]{0:T(128)}, u32[]{:S(2)}) %copy-start.6) | copy-done | bytes 40
  0.7 0.2 copy-done.4
  0.9 0.1 copy-done.3
  1.0 1.0 %shard_map.119.latent = f32[4,16,512]{2,1,0:T(8,128)S(1)} custom-call(s32[4]{0:T(128)S(1)} %copy-done.6, bf16[4,16,576]{2,1,0:T(8,128)(2,1)S(1)} %copy-done.4, bf16[4,32,576]{2,1,0:T(8,128)(2,1)S(1)} %copy-done.3, bf16[64,64]{1,0:T(8,128)(2,1)S(1)} %shard_map.118.pick), custom_call_target="tpu_custom_call" | custom-call | flops 1000000000 | bytes 1000000 | tf_op jit(solution)/shard_map/pallas_call | solution.py:31
  2.0 0.0 copy-done.2
  2.0 0.0 slice-start.13
  2.0 0.0 slice-start.4
  2.0 0.0 slice-start.8
  2.0 1.0 %shard_map.120.own = bf16[16,1024]{1,0:T(8,128)(2,1)S(1)} custom-call(s32[4,4]{1,0:T(4,128)S(1)} %copy-done, f32[4,16,512]{2,1,0:T(8,128)S(1)} %shard_map.119.latent, bf16[16,512,128]{2,1,0:T(8,128)(2,1)S(1)} %copy-done.2, bf16[4,1792]{1,0:T(4,128)(2,1)S(1)} %copy-done.5), custom_call_target="tpu_custom_call" | custom-call | flops 20000000000 | bytes 1000000 | tf_op jit(solution)/shard_map/pallas_call | solution.py:31
  3.0 0.0 copy-start.7
  3.0 0.0 slice-start.5
  3.1 0.0 slice-start.6
  3.1 0.0 slice-start.7
  3.1 0.0 slice-start.9
  3.1 3.1 %collective-permute-start = (bf16[16,1024]{1,0:T(8,128)(2,1)S(1)}, bf16[16,1024]{1,0:T(8,128)(2,1)S(1)}, u32[]{:S(2)}, u32[]{:S(2)}) collective-permute-start(bf16[16,1024]{1,0:T(8,128)(2,1)S(1)} %shard_map.120.own), channel_id=1, source_target_pairs={{0,4},{4,0},{8,12},{12,8},{1,5},{5,1},{9,13},{13,9},{2,6},{6,2},{1... | collective-permute-start | bytes 98312 | tf_op jit(solution)/shard_map/ppermute | solution.py:390
  6.2 2.6 %collective-permute-start.1 = (bf16[16,1024]{1,0:T(8,128)(2,1)S(1)}, bf16[16,1024]{1,0:T(8,128)(2,1)S(1)}, u32[]{:S(2)}, u32[]{:S(2)}) collective-permute-start(bf16[16,1024]{1,0:T(8,128)(2,1)S(1)} %shard_map.120.own), channel_id=1, source_target_pairs={{0,8},{4,12},{8,0},{12,4},{1,9},{5,13},{9,1},{13,5},{2,10},{6,14},... | collective-permute-start | bytes 98312 | tf_op jit(solution)/shard_map/ppermute | solution.py:390
  8.8 0.0 collective-permute-start.2
  8.8 0.0 collective-permute-done.got1
  8.8 2.8 %collective-permute-done.1.got2 = bf16[16,1024]{1,0:T(8,128)(2,1)S(1)} collective-permute-done((bf16[16,1024]{1,0:T(8,128)(2,1)S(1)}, bf16[16,1024]{1,0:T(8,128)(2,1)S(1)}, u32[]{:S(2)}, u32[]{:S(2)}) %collective-permute-start.1) | collective-permute-done | bytes 32800 | tf_op jit(solution)/shard_map/ppermute | solution.py:390
  11.6 2.9 %collective-permute-done.2.got3 = bf16[16,1024]{1,0:T(8,128)(2,1)S(1)} collective-permute-done((bf16[16,1024]{1,0:T(8,128)(2,1)S(1)}, bf16[16,1024]{1,0:T(8,128)(2,1)S(1)}, u32[]{:S(2)}, u32[]{:S(2)}) %collective-permute-start.2) | collective-permute-done | bytes 32800 | tf_op jit(solution)/shard_map/ppermute | solution.py:390
  14.5 1.2 %shard_map.121 = (f32[16,1792]{1,0:T(8,128)S(1)}, bf16[32,1024]{1,0:T(8,128)(2,1)S(1)}) custom-call(bf16[64,64]{1,0:T(8,128)(2,1)S(1)} %shard_map.118.pick, bf16[16,1024]{1,0:T(8,128)(2,1)S(1)} %shard_map.120.own, bf16[16,1024]{1,0:T(8,128)(2,1)S(1)} %collective-permute-done.got1, bf16[16,1024]{1,0:T(8,128)(2,1)S(1)} %collective-permute-done.1.got2, ...), custom_call_target="tpu_custom_call" | custom-call | flops 60000002048 | bytes 1000000 | tf_op jit(solution)/shard_map/pallas_call | solution.py:31
  15.7 1.3 %collective-permute-done.4.two = f32[16,1792]{1,0:T(8,128)S(1)} collective-permute-done((f32[16,1792]{1,0:T(8,128)S(1)}, f32[16,1792]{1,0:T(8,128)S(1)}, u32[]{:S(2)}, u32[]{:S(2)}) %collective-permute-start.4) | collective-permute-done | bytes 114720 | tf_op jit(solution)/shard_map/ppermute | solution.py:398
  17.0 1.6 %collective-permute-start.5 = (bf16[16,1792]{1,0:T(8,128)(2,1)S(1)}, bf16[16,1792]{1,0:T(8,128)(2,1)S(1)}, u32[]{:S(2)}, u32[]{:S(2)}) collective-permute-start(bf16[16,1792]{1,0:T(8,128)(2,1)S(1)} %shard_map.123.one), channel_id=1, source_target_pairs={{0,2},{1,3},{2,0},{3,1},{4,6},{5,7},{6,4},{7,5},{8,10},{9,11},{10,... | collective-permute-start | bytes 172040 | tf_op jit(solution)/shard_map/ppermute | solution.py:401
  18.6 1.5 %collective-permute-start.3 = (bf16[32,1024]{1,0:T(8,128)(2,1)S(1)}, bf16[32,1024]{1,0:T(8,128)(2,1)S(1)}, u32[]{:S(2)}, u32[]{:S(2)}) collective-permute-start(bf16[32,1024]{1,0:T(8,128)(2,1)S(1)} %get-tuple-element.14.extra), channel_id=1, source_target_pairs={{0,16},{16,0},{1,17},{17,1},{2,18},{18,2},{3,19},{19,3},{4,20},{20... | collective-permute-start | bytes 196616 | tf_op jit(solution)/shard_map/ppermute | solution.py:399
  20.1 1.2 %collective-permute-done.5.two = bf16[16,1792]{1,0:T(8,128)(2,1)S(1)} collective-permute-done((bf16[16,1792]{1,0:T(8,128)(2,1)S(1)}, bf16[16,1792]{1,0:T(8,128)(2,1)S(1)}, u32[]{:S(2)}, u32[]{:S(2)}) %collective-permute-start.5) | collective-permute-done | bytes 57376 | tf_op jit(solution)/shard_map/ppermute | solution.py:401
  21.3 0.7 %collective-permute-start.6 = (bf16[16,1792]{1,0:T(8,128)(2,1)S(1)}, bf16[16,1792]{1,0:T(8,128)(2,1)S(1)}, u32[]{:S(2)}, u32[]{:S(2)}) collective-permute-start(bf16[16,1792]{1,0:T(8,128)(2,1)S(1)} %shard_map.124), channel_id=1, source_target_pairs={{0,0},{1,4},{2,8},{3,12},{4,1},{5,5},{6,9},{7,13},{8,2},{9,6},{10,... | collective-permute-start | bytes 172040 | tf_op jit(solution)/shard_map/ppermute | solution.py:403
  22.0 1.6 %collective-permute-start.7 = (bf16[16,1792]{1,0:T(8,128)(2,1)S(1)}, bf16[16,1792]{1,0:T(8,128)(2,1)S(1)}, u32[]{:S(2)}, u32[]{:S(2)}) collective-permute-start(bf16[16,1792]{1,0:T(8,128)(2,1)S(1)} %shard_map.124), channel_id=1, source_target_pairs={{0,16},{1,20},{2,24},{3,28},{4,17},{5,21},{6,25},{7,29},{8,18},{9,... | collective-permute-start | bytes 172040 | tf_op jit(solution)/shard_map/ppermute | solution.py:404
  23.5 0.3 shard_map.122
  23.9 0.0 collective-permute-done.6.same
  23.9 2.3 %collective-permute-done.7.other = bf16[16,1792]{1,0:T(8,128)(2,1)S(1)} collective-permute-done((bf16[16,1792]{1,0:T(8,128)(2,1)S(1)}, bf16[16,1792]{1,0:T(8,128)(2,1)S(1)}, u32[]{:S(2)}, u32[]{:S(2)}) %collective-permute-start.7) | collective-permute-done | bytes 57376 | tf_op jit(solution)/shard_map/ppermute | solution.py:404
  26.3 0.0 slice-start
  26.3 0.0 slice-start.1
  26.3 2.2 %shard_map.125 = (f32[16,4224]{1,0:T(8,128)S(1)}, bf16[16,1792]{1,0:T(8,128)(2,1)S(1)}, bf16[4,1792]{1,0:T(4,128)(2,1)S(1)}) custom-call(f32[32,1792]{1,0:T(8,128)S(1)} %get-tuple-element.15.known, bf16[16,1792]{1,0:T(8,128)(2,1)S(1)} %collective-permute-done.6.same, bf16[16,1792]{1,0:T(8,128)(2,1)S(1)} %collective-permute-done.7.other, ...), custom_call_target="tpu_custom_call" | custom-call | flops 20000000000 | bytes 1000000 | tf_op jit(solution)/shard_map/pallas_call | solution.py:31
  28.5 1.1 %collective-permute-start.8 = (f32[16,4224]{1,0:T(8,128)S(1)}, f32[16,4224]{1,0:T(8,128)S(1)}, u32[]{:S(2)}, u32[]{:S(2)}) collective-permute-start(f32[16,4224]{1,0:T(8,128)S(1)} %get-tuple-element.20), channel_id=1, source_target_pairs={{0,1},{1,0},{2,3},{3,2},{4,5},{5,4},{6,7},{7,6},{8,9},{9,8},{10,11... | collective-permute-start | bytes 811016 | tf_op jit(solution)/shard_map/ppermute | solution.py:422
  29.6 2.0 %shard_map.126.own = f32[16,4224]{1,0:T(8,128)S(1)} custom-call(bf16[16,1792]{1,0:T(8,128)(2,1)S(1)} %get-tuple-element.19.mine, f32[1,1792]{1,0:T(1,128)S(1)} %reshape.3.gain, bf16[16,1792,256]{2,1,0:T(8,128)(2,1)S(1)} %bitcast.3, bf16[16,1792,256]{2,1,0:T(8,128)(2,1)S(1)} %bitcast.5), custom_call_target="tpu_custom_call" | custom-call | flops 20000000000 | bytes 1000000 | tf_op jit(solution)/shard_map/pallas_call | solution.py:31
  31.6 0.1 shard_map.127
  31.7 5.7 %collective-permute-start.9 = (bf16[16,4224]{1,0:T(8,128)(2,1)S(1)}, bf16[16,4224]{1,0:T(8,128)(2,1)S(1)}, u32[]{:S(2)}, u32[]{:S(2)}) collective-permute-start(bf16[16,4224]{1,0:T(8,128)(2,1)S(1)} %get-tuple-element.22), channel_id=1, source_target_pairs={{0,2},{1,3},{2,0},{3,1},{4,6},{5,7},{6,4},{7,5},{8,10},{9,11},{10,... | collective-permute-start | bytes 405512 | tf_op jit(solution)/shard_map/ppermute | solution.py:433
  37.4 4.2 %collective-permute-done.9.got = bf16[16,4224]{1,0:T(8,128)(2,1)S(1)} collective-permute-done((bf16[16,4224]{1,0:T(8,128)(2,1)S(1)}, bf16[16,4224]{1,0:T(8,128)(2,1)S(1)}, u32[]{:S(2)}, u32[]{:S(2)}) %collective-permute-start.9) | collective-permute-done | bytes 135200 | tf_op jit(solution)/shard_map/ppermute | solution.py:433
  41.6 0.1 shard_map.128.act
  41.8 0.0 copy-start.1
  41.8 0.1 collective-permute-start.10
  41.9 1.1 %shard_map.129.done = bf16[16,1792]{1,0:T(8,128)(2,1)S(1)} custom-call(bf16[16,2048]{1,0:T(8,128)(2,1)S(1)} %shard_map.128.act, bf16[16,256,1792]{2,1,0:T(8,128)(2,1)S(1)} %bitcast.1), custom_call_target="tpu_custom_call" | custom-call | tf_op jit(solution)/shard_map/pallas_call | solution.py:31
  43.0 0.1 collective-permute-done.10.act
  43.1 1.9 %shard_map.130 = bf16[8,8,896]{2,1,0:T(8,128)(2,1)} custom-call(bf16[16,2048]{1,0:T(8,128)(2,1)S(1)} %collective-permute-done.10.act, bf16[16,256,1792]{2,1,0:T(8,128)(2,1)S(1)} %bitcast.1, bf16[16,1792]{1,0:T(8,128)(2,1)S(1)} %shard_map.129.done), custom_call_target="tpu_custom_call" | custom-call | tf_op jit(solution)/shard_map/pallas_call | solution.py:31
  45.0 5.0 %all-to-all-start = ((bf16[8,8,896]{2,1,0:T(8,128)(2,1)}), bf16[8,8,896]{2,1,0:T(8,128)(2,1)S(1)}, u32[]{:S(2)}, u32[]{:S(2)}) async-start(bf16[8,8,896]{2,1,0:T(8,128)(2,1)} %shard_map.130), calls=%async_computation | async-start | bytes 229376 | tf_op jit(solution)/shard_map/all_to_all | solution.py:443
  50.0 0.7 %shard_map.131.mix = bf16[24,64]{1,0:T(8,128)(2,1)S(1)} custom-call(s32[4,4]{1,0:T(4,128)S(1)} %copy-done, f32[4,4]{1,0:T(4,128)S(1)} %copy-done.1), custom_call_target="tpu_custom_call" | custom-call | tf_op jit(solution)/shard_map/pallas_call | solution.py:31
  50.8 6.7 %all-to-all-done.back = bf16[8,8,896]{2,1,0:T(8,128)(2,1)S(1)} async-done(((bf16[8,8,896]{2,1,0:T(8,128)(2,1)}), bf16[8,8,896]{2,1,0:T(8,128)(2,1)S(1)}, u32[]{:S(2)}, u32[]{:S(2)}) %all-to-all-start) | async-done | bytes 114720 | tf_op jit(solution)/shard_map/all_to_all | solution.py:443
  57.4 0.7 %shard_map.132 = bf16[4,1792]{1,0:T(4,128)(2,1)} custom-call(bf16[4,1792]{1,0:T(4,128)(2,1)S(1)} %get-tuple-element.18.state, bf16[8,8,896]{2,1,0:T(8,128)(2,1)S(1)} %all-to-all-done.back, bf16[24,64]{1,0:T(8,128)(2,1)S(1)} %shard_map.131.mix), custom_call_target="tpu_custom_call" | custom-call | tf_op jit(solution)/shard_map/pallas_call | solution.py:31
  (40 shorter events, 0.1 us)
Async XLA Ops:
  0.0 0.7 %copy-start.6 = (s32[4]{0:T(128)S(1)}, s32[4]{0:T(128)}, u32[]{:S(2)}) copy-start(s32[4]{0:T(128)} %lengths.1) | copy-start | bytes 52
  0.0 0.9 %copy-start.4 = (bf16[4,16,576]{2,1,0:T(8,128)(2,1)S(1)}, bf16[4,16,576]{2,1,0:T(8,128)(2,1)}, u32[]{:S(2)}) copy-start(bf16[4,16,576]{2,1,0:T(8,128)(2,1)} %queries.1) | copy-start | bytes 221188
  0.0 1.0 %copy-start.3 = (bf16[4,32,576]{2,1,0:T(8,128)(2,1)S(1)}, bf16[4,32,576]{2,1,0:T(8,128)(2,1)}, u32[]{:S(2)}) copy-start(bf16[4,32,576]{2,1,0:T(8,128)(2,1)} %cache.1) | copy-start | bytes 442372
  0.0 2.0 %copy-start = (s32[4,4]{1,0:T(4,128)S(1)}, s32[4,4]{1,0:T(4,128)}, u32[]{:S(2)}) copy-start(s32[4,4]{1,0:T(4,128)} %ids.3) | copy-start | bytes 196
  0.0 2.0 %copy-start.2 = (bf16[16,512,128]{2,1,0:T(8,128)(2,1)S(1)}, bf16[16,512,128]{2,1,0:T(8,128)(2,1)}, u32[]{:S(2)}) copy-start(bf16[16,512,128]{2,1,0:T(8,128)(2,1)} %w_uv.1) | copy-start | bytes 6291460
  0.0 2.0 %copy-start.5 = (bf16[4,1792]{1,0:T(4,128)(2,1)S(1)}, bf16[4,1792]{1,0:T(4,128)(2,1)}, u32[]{:S(2)}) copy-start(bf16[4,1792]{1,0:T(4,128)(2,1)} %residual.1) | copy-start | bytes 43012
  1.0 13.5 %slice-start.12 = ((s8[7340032]{0:T(1024)(128)(4,1)}), s8[4194304]{0:T(1024)(128)(4,1)S(1)}, s32[]{:S(2)}) async-start(s8[7340032]{0:T(1024)(128)(4,1)} %bitcast.6), calls=%async_computation.13 | async-start | bytes 8388608
  2.0 12.5 %slice-start.13 = ((s8[7340032]{0:T(1024)(128)(4,1)}), s8[3145728]{0:T(1024)(128)(4,1)S(1)}, s32[]{:S(2)}) async-start(s8[7340032]{0:T(1024)(128)(4,1)} %bitcast.6), calls=%async_computation.14 | async-start | bytes 6291456
  2.0 24.2 %slice-start.4 = ((s8[14680064]{0:T(1024)(128)(4,1)}), s8[4194304]{0:T(1024)(128)(4,1)S(1)}, s32[]{:S(2)}) async-start(s8[14680064]{0:T(1024)(128)(4,1)} %bitcast.2), calls=%async_computation.5 | async-start | bytes 8388608
  2.0 24.2 %slice-start.8 = ((s8[14680064]{0:T(1024)(128)(4,1)}), s8[4194304]{0:T(1024)(128)(4,1)S(1)}, s32[]{:S(2)}) async-start(s8[14680064]{0:T(1024)(128)(4,1)} %bitcast.4), calls=%async_computation.9 | async-start | bytes 8388608
  3.0 20.5 %copy-start.7 = (f32[1792]{0:T(1024)S(1)}, f32[1792]{0:T(1024)}, u32[]{:S(2)}) copy-start(f32[1792]{0:T(1024)} %param.18) | copy-start | bytes 21508
  3.0 23.2 %slice-start.5 = ((s8[14680064]{0:T(1024)(128)(4,1)}), s8[4194304]{0:T(1024)(128)(4,1)S(1)}, s32[]{:S(2)}) async-start(s8[14680064]{0:T(1024)(128)(4,1)} %bitcast.2), calls=%async_computation.6 | async-start | bytes 8388608
  3.1 23.2 %slice-start.6 = ((s8[14680064]{0:T(1024)(128)(4,1)}), s8[4194304]{0:T(1024)(128)(4,1)S(1)}, s32[]{:S(2)}) async-start(s8[14680064]{0:T(1024)(128)(4,1)} %bitcast.2), calls=%async_computation.7 | async-start | bytes 8388608
  3.1 23.2 %slice-start.7 = ((s8[14680064]{0:T(1024)(128)(4,1)}), s8[2097152]{0:T(1024)(128)(4,1)S(1)}, s32[]{:S(2)}) async-start(s8[14680064]{0:T(1024)(128)(4,1)} %bitcast.2), calls=%async_computation.8 | async-start | bytes 4194304
  3.1 23.2 %slice-start.9 = ((s8[14680064]{0:T(1024)(128)(4,1)}), s8[4194304]{0:T(1024)(128)(4,1)S(1)}, s32[]{:S(2)}) async-start(s8[14680064]{0:T(1024)(128)(4,1)} %bitcast.4), calls=%async_computation.10 | async-start | bytes 8388608
  3.1 23.2 %slice-start.10 = ((s8[14680064]{0:T(1024)(128)(4,1)}), s8[4194304]{0:T(1024)(128)(4,1)S(1)}, s32[]{:S(2)}) async-start(s8[14680064]{0:T(1024)(128)(4,1)} %bitcast.4), calls=%async_computation.11 | async-start | bytes 8388608
  3.1 23.2 %slice-start.11 = ((s8[14680064]{0:T(1024)(128)(4,1)}), s8[2097152]{0:T(1024)(128)(4,1)S(1)}, s32[]{:S(2)}) async-start(s8[14680064]{0:T(1024)(128)(4,1)} %bitcast.4), calls=%async_computation.12 | async-start | bytes 4194304
  3.1 5.7 %collective-permute-start = (bf16[16,1024]{1,0:T(8,128)(2,1)S(1)}, bf16[16,1024]{1,0:T(8,128)(2,1)S(1)}, u32[]{:S(2)}, u32[]{:S(2)}) collective-permute-start(bf16[16,1024]{1,0:T(8,128)(2,1)S(1)} %shard_map.120.own), channel_id=1, source_target_pairs={{0,4},{4,0},{8,12},{12,8},{1,5},{5,1},{9,13},{13,9},{2,6},{6,2},{1... | collective-permute-start | bytes 98312 | tf_op jit(solution)/shard_map/ppermute | solution.py:390
  6.2 5.4 %collective-permute-start.1 = (bf16[16,1024]{1,0:T(8,128)(2,1)S(1)}, bf16[16,1024]{1,0:T(8,128)(2,1)S(1)}, u32[]{:S(2)}, u32[]{:S(2)}) collective-permute-start(bf16[16,1024]{1,0:T(8,128)(2,1)S(1)} %shard_map.120.own), channel_id=1, source_target_pairs={{0,8},{4,12},{8,0},{12,4},{1,9},{5,13},{9,1},{13,5},{2,10},{6,14},... | collective-permute-start | bytes 98312 | tf_op jit(solution)/shard_map/ppermute | solution.py:390
  8.8 5.7 %collective-permute-start.2 = (bf16[16,1024]{1,0:T(8,128)(2,1)S(1)}, bf16[16,1024]{1,0:T(8,128)(2,1)S(1)}, u32[]{:S(2)}, u32[]{:S(2)}) collective-permute-start(bf16[16,1024]{1,0:T(8,128)(2,1)S(1)} %shard_map.120.own), channel_id=1, source_target_pairs={{0,12},{4,8},{8,4},{12,0},{1,13},{5,9},{9,5},{13,1},{2,14},{6,10},... | collective-permute-start | bytes 98312 | tf_op jit(solution)/shard_map/ppermute | solution.py:390
  15.7 1.3 %collective-permute-start.4 = (f32[16,1792]{1,0:T(8,128)S(1)}, f32[16,1792]{1,0:T(8,128)S(1)}, u32[]{:S(2)}, u32[]{:S(2)}) collective-permute-start(f32[16,1792]{1,0:T(8,128)S(1)} %get-tuple-element.16.one), channel_id=1, source_target_pairs={{0,1},{1,0},{2,3},{3,2},{4,5},{5,4},{6,7},{7,6},{8,9},{9,8},{10,11... | collective-permute-start | bytes 344072 | tf_op jit(solution)/shard_map/ppermute | solution.py:398
  17.0 4.2 %collective-permute-start.5 = (bf16[16,1792]{1,0:T(8,128)(2,1)S(1)}, bf16[16,1792]{1,0:T(8,128)(2,1)S(1)}, u32[]{:S(2)}, u32[]{:S(2)}) collective-permute-start(bf16[16,1792]{1,0:T(8,128)(2,1)S(1)} %shard_map.123.one), channel_id=1, source_target_pairs={{0,2},{1,3},{2,0},{3,1},{4,6},{5,7},{6,4},{7,5},{8,10},{9,11},{10,... | collective-permute-start | bytes 172040 | tf_op jit(solution)/shard_map/ppermute | solution.py:401
  18.6 4.9 %collective-permute-start.3 = (bf16[32,1024]{1,0:T(8,128)(2,1)S(1)}, bf16[32,1024]{1,0:T(8,128)(2,1)S(1)}, u32[]{:S(2)}, u32[]{:S(2)}) collective-permute-start(bf16[32,1024]{1,0:T(8,128)(2,1)S(1)} %get-tuple-element.14.extra), channel_id=1, source_target_pairs={{0,16},{16,0},{1,17},{17,1},{2,18},{18,2},{3,19},{19,3},{4,20},{20... | collective-permute-start | bytes 196616 | tf_op jit(solution)/shard_map/ppermute | solution.py:399
  21.3 2.6 %collective-permute-start.6 = (bf16[16,1792]{1,0:T(8,128)(2,1)S(1)}, bf16[16,1792]{1,0:T(8,128)(2,1)S(1)}, u32[]{:S(2)}, u32[]{:S(2)}) collective-permute-start(bf16[16,1792]{1,0:T(8,128)(2,1)S(1)} %shard_map.124), channel_id=1, source_target_pairs={{0,0},{1,4},{2,8},{3,12},{4,1},{5,5},{6,9},{7,13},{8,2},{9,6},{10,... | collective-permute-start | bytes 172040 | tf_op jit(solution)/shard_map/ppermute | solution.py:403
  22.0 4.2 %collective-permute-start.7 = (bf16[16,1792]{1,0:T(8,128)(2,1)S(1)}, bf16[16,1792]{1,0:T(8,128)(2,1)S(1)}, u32[]{:S(2)}, u32[]{:S(2)}) collective-permute-start(bf16[16,1792]{1,0:T(8,128)(2,1)S(1)} %shard_map.124), channel_id=1, source_target_pairs={{0,16},{1,20},{2,24},{3,28},{4,17},{5,21},{6,25},{7,29},{8,18},{9,... | collective-permute-start | bytes 172040 | tf_op jit(solution)/shard_map/ppermute | solution.py:404
  26.3 15.6 %slice-start = ((s8[14680064]{0:T(1024)(128)(4,1)}), s8[2097152]{0:T(1024)(128)(4,1)S(1)}, s32[]{:S(2)}) async-start(s8[14680064]{0:T(1024)(128)(4,1)} %bitcast), calls=%async_computation.1 | async-start | bytes 4194304
  26.3 15.6 %slice-start.1 = ((s8[14680064]{0:T(1024)(128)(4,1)}), s8[4194304]{0:T(1024)(128)(4,1)S(1)}, s32[]{:S(2)}) async-start(s8[14680064]{0:T(1024)(128)(4,1)} %bitcast), calls=%async_computation.2 | async-start | bytes 8388608
  28.5 3.2 %collective-permute-start.8 = (f32[16,4224]{1,0:T(8,128)S(1)}, f32[16,4224]{1,0:T(8,128)S(1)}, u32[]{:S(2)}, u32[]{:S(2)}) collective-permute-start(f32[16,4224]{1,0:T(8,128)S(1)} %get-tuple-element.20), channel_id=1, source_target_pairs={{0,1},{1,0},{2,3},{3,2},{4,5},{5,4},{6,7},{7,6},{8,9},{9,8},{10,11... | collective-permute-start | bytes 811016 | tf_op jit(solution)/shard_map/ppermute | solution.py:422
  29.6 12.3 %slice-start.2 = ((s8[14680064]{0:T(1024)(128)(4,1)}), s8[4194304]{0:T(1024)(128)(4,1)S(1)}, s32[]{:S(2)}) async-start(s8[14680064]{0:T(1024)(128)(4,1)} %bitcast), calls=%async_computation.3 | async-start | bytes 8388608
  29.6 12.3 %slice-start.3 = ((s8[14680064]{0:T(1024)(128)(4,1)}), s8[4194304]{0:T(1024)(128)(4,1)S(1)}, s32[]{:S(2)}) async-start(s8[14680064]{0:T(1024)(128)(4,1)} %bitcast), calls=%async_computation.4 | async-start | bytes 8388608
  31.7 9.9 %collective-permute-start.9 = (bf16[16,4224]{1,0:T(8,128)(2,1)S(1)}, bf16[16,4224]{1,0:T(8,128)(2,1)S(1)}, u32[]{:S(2)}, u32[]{:S(2)}) collective-permute-start(bf16[16,4224]{1,0:T(8,128)(2,1)S(1)} %get-tuple-element.22), channel_id=1, source_target_pairs={{0,2},{1,3},{2,0},{3,1},{4,6},{5,7},{6,4},{7,5},{8,10},{9,11},{10,... | collective-permute-start | bytes 405512 | tf_op jit(solution)/shard_map/ppermute | solution.py:433
  41.8 8.2 %copy-start.1 = (f32[4,4]{1,0:T(4,128)S(1)}, f32[4,4]{1,0:T(4,128)}, u32[]{:S(2)}) copy-start(f32[4,4]{1,0:T(4,128)} %weights.1) | copy-start | bytes 196
  41.8 1.3 %collective-permute-start.10 = (bf16[16,2048]{1,0:T(8,128)(2,1)S(1)}, bf16[16,2048]{1,0:T(8,128)(2,1)S(1)}, u32[]{:S(2)}, u32[]{:S(2)}) collective-permute-start(bf16[16,2048]{1,0:T(8,128)(2,1)S(1)} %shard_map.128.act), channel_id=1, source_target_pairs={{0,1},{1,0},{2,3},{3,2},{4,5},{5,4},{6,7},{7,6},{8,9},{9,8},{10,11... | collective-permute-start | bytes 196616 | tf_op jit(solution)/shard_map/ppermute | solution.py:435
  45.0 12.4 %all-to-all-start = ((bf16[8,8,896]{2,1,0:T(8,128)(2,1)}), bf16[8,8,896]{2,1,0:T(8,128)(2,1)S(1)}, u32[]{:S(2)}, u32[]{:S(2)}) async-start(bf16[8,8,896]{2,1,0:T(8,128)(2,1)} %shard_map.130), calls=%async_computation | async-start | bytes 229376 | tf_op jit(solution)/shard_map/all_to_all | solution.py:443

commit v3 on v2

--- a/solution.py
+++ b/solution.py
@@ -1,3 +1,5 @@
+import functools
+
 import jax
 import jax.numpy as jnp
 from jax import lax
@@ -202,32 +204,32 @@
     ).astype(bf16)
 
 
-def expert_partial(rows, gain, w_gate, w_up, expert, store):
-    square = jnp.sum(rows * rows, axis=1, keepdims=True)
-    scaled = (rows * gain[...]).astype(bf16)
-    hid = w_gate.shape[2]
-    for p in range(HSPLIT):
-        at = expert * HSPLIT + p
-        store(p * hid, dot(scaled, w_gate[at]))
-        store((HSPLIT + p) * hid, dot(scaled, w_up[at]))
+def three_terms(square):
     high = square.astype(bf16).astype(f32)
     middle = (square - high).astype(bf16).astype(f32)
     low = square - high - middle
-    lane = lax.broadcasted_iota(jnp.int32, (rows.shape[0], 128), 1)
-    store(
-        2 * HSPLIT * hid,
-        jnp.where(
-            lane == 0,
-            high,
-            jnp.where(lane == 1, middle, jnp.where(lane == 2, low, 0.0)),
-        ),
-    )
-
-
-def experts_away_body(known, same, other, choice, gain, w_gate, w_up, out, mine, state):
+    lane = lax.broadcasted_iota(jnp.int32, (square.shape[0], 128), 1)
+    return jnp.where(
+        lane == 0, high, jnp.where(lane == 1, middle, jnp.where(lane == 2, low, 0.0))
+    )
+
+
+def expert_partial(rows, gain, w_gate, w_up, expert, part, out):
+    scaled = (rows * gain[...]).astype(bf16)
+    hid = w_gate.shape[2]
+    count = HSPLIT // 2
+    for p in range(count):
+        at = expert * HSPLIT + part * count + p
+        out[:, p * hid : (p + 1) * hid] = dot(scaled, w_gate[at])
+        out[:, (count + p) * hid : (count + p + 1) * hid] = dot(scaled, w_up[at])
+    if part == 0:
+        out[:, 2 * count * hid :] = three_terms(jnp.sum(rows * rows, axis=1, keepdims=True))
+
+
+def experts_away_body(known, same, other, choice, gain, w_gate, w_up, out0, out1, mine, state):
     core = lax.axis_index("tp") % 2
     block = same.shape[0]
-    lines = out.shape[0]
+    lines = out0.shape[0]
     hidden = jnp.concatenate(
         [
             (known[:block] + same[...].astype(f32)).astype(bf16),
@@ -240,47 +242,36 @@
     mine[...] = jnp.where(core == 0, first, second).astype(bf16)
     state[...] = table[2 * lines : 2 * lines + state.shape[0]].astype(bf16)
 
-    def store(lane, value):
-        out[:, lane : lane + value.shape[1]] = value
-
     rows = jnp.where(core == 0, second, first)
-    expert_partial(rows, gain, w_gate, w_up, 1 - core, store)
-
-
-def experts_own_body(mine, gain, w_gate, w_up, out):
+    expert_partial(rows, gain, w_gate, w_up, 1 - core, 0, out0)
+    expert_partial(rows, gain, w_gate, w_up, 1 - core, 1, out1)
+
+
+def experts_own_body(part, mine, gain, w_gate, w_up, out):
     core = lax.axis_index("tp") % 2
-
-    def store(lane, value):
-        out[:, lane : lane + value.shape[1]] = value
-
-    expert_partial(mine[...].astype(f32), gain, w_gate, w_up, core, store)
-
-
-def merge_body(own, got, total, send):
+    expert_partial(mine[...].astype(f32), gain, w_gate, w_up, core, part, out)
+
+
+def merge_body(tail, own, got, total, send):
     whole = own[...] + got[...]
     total[...] = whole
-    tail = whole.shape[1] - 128
     send[:, :tail] = whole[:, :tail].astype(bf16)
-    square = jnp.sum(whole[:, tail:], axis=1, keepdims=True)
-    high = square.astype(bf16).astype(f32)
-    middle = (square - high).astype(bf16).astype(f32)
-    low = square - high - middle
-    lane = lax.broadcasted_iota(jnp.int32, (whole.shape[0], 128), 1)
-    send[:, tail:] = jnp.where(
-        lane == 0,
-        high,
-        jnp.where(lane == 1, middle, jnp.where(lane == 2, low, 0.0)),
-    ).astype(bf16)
-
-
-def act_body(total, got, out):
-    hidden = out.shape[1]
-    whole = total[...] + got[...].astype(f32)
-    square = jnp.sum(whole[:, 2 * hidden :], axis=1, keepdims=True)
-    inv_rms = lax.rsqrt(square / D + norm_eps)
-    gate = whole[:, :hidden] * inv_rms
-    up = whole[:, hidden : 2 * hidden] * inv_rms
-    out[...] = (gate / (1.0 + jnp.exp(-gate)) * up).astype(bf16)
+    if whole.shape[1] > tail:
+        square = jnp.sum(whole[:, tail:], axis=1, keepdims=True)
+        send[:, tail:] = three_terms(square).astype(bf16)
+
+
+def act_body(total0, got0, total1, got1, out):
+    part = out.shape[1] // 2
+    inv_rms = None
+    for i, (total, got) in enumerate(((total0, got0), (total1, got1))):
+        whole = total[...] + got[...].astype(f32)
+        if i == 0:
+            square = jnp.sum(whole[:, 2 * part :], axis=1, keepdims=True)
+            inv_rms = lax.rsqrt(square / D + norm_eps)
+        gate = whole[:, :part] * inv_rms
+        up = whole[:, part : 2 * part] * inv_rms
+        out[:, i * part : (i + 1) * part] = (gate / (1.0 + jnp.exp(-gate)) * up).astype(bf16)
 
 
 def down_one(act, w_down, expert):
@@ -411,27 +402,32 @@
     (mix,) = call(
         mix_body, [((6 * rows, groups * 2 * slots), bf16)], (expert_ids, expert_weights), [SMEM] * 2
     )
-    wide = 2 * hidden + 128
-    away, mine, state = call(
+    wides = (hidden + 128, hidden)
+    away0, away1, mine, state = call(
         experts_away_body,
-        [((lines, wide), f32), ((lines, columns), bf16), ((rows, columns), bf16)],
+        [((lines, w), f32) for w in wides] + [((lines, columns), bf16), ((rows, columns), bf16)],
         (known, same, cross, choice, gain, w_gate, w_up),
         [VMEM] * 7,
         cost=COSTS[6],
     )
-    away = lax.ppermute(away, "tp", swap("tp", 1))
-    (own,) = call(
-        experts_own_body,
-        [((lines, wide), f32)],
-        (mine, gain, w_gate, w_up),
-        [VMEM] * 4,
-        cost=COSTS[7],
-    )
-    total, send = call(
-        merge_body, [((lines, wide), f32), ((lines, wide), bf16)], (own, away), [VMEM] * 2
-    )
-    got = lax.ppermute(send, "tp", swap("tp", 2))
-    (act,) = call(act_body, [((lines, hidden), bf16)], (total, got), [VMEM] * 2)
+    done = []
+    for i, away in enumerate((away0, away1)):
+        away = lax.ppermute(away, "tp", swap("tp", 1))
+        (own,) = call(
+            functools.partial(experts_own_body, i),
+            [((lines, wides[i]), f32)],
+            (mine, gain, w_gate, w_up),
+            [VMEM] * 4,
+            cost=COSTS[7],
+        )
+        total, send = call(
+            functools.partial(merge_body, hidden),
+            [((lines, wides[i]), f32), ((lines, wides[i]), bf16)],
+            (own, away),
+            [VMEM] * 2,
+        )
+        done += [total, lax.ppermute(send, "tp", swap("tp", 2))]
+    (act,) = call(act_body, [((lines, hidden), bf16)], tuple(done), [VMEM] * 4)
     act_away = lax.ppermute(act, "tp", swap("tp", 1))
     (done,) = call(down_own_body, [((lines, columns), bf16)], (act, w_down), [VMEM] * 2)
     (back,) = call(

time: 58.4 us -> 57.8 us (0.990)
  starting transfers between devices: 22.9 us -> 21.8 us
    all_to_all x1, starting transfers between devices: 5.03 us -> 3.62 us  [local(): lax.all_to_all(back, ('sec', 'ep'), split_axis=0, concat_axis=0, tiled=True)]
    ppermute x1 -> x2, starting transfers between devices: 5.67 us -> 6.01 us  [local(): done += [total, lax.ppermute(send, 'tp', swap('tp', 2))]]
    pallas_call x15 -> x17, Pallas kernels: 12.4 us -> 12.5 us  [call(): pl.pallas_call(body, out_shape=[jax.ShapeDtypeStruct(s, d) for s, d in ou...]
    ppermute x1 -> x2, waiting for transfers between devices: 4.24 us -> 4.24 us  [local(): done += [total, lax.ppermute(send, 'tp', swap('tp', 2))]]
  transfers between devices with their start and end apart: 12 -> 14, of which waited for: 8 -> 9; matrix products, arithmetic and copies ran while one was open for 0% -> 0% of each run, Pallas kernels for 7% -> 8%
where the time goes in v3:
time: 57.8 us; the launch traced here: 57.5 us
  starting transfers between devices  21.8 us (38%)
  waiting for transfers between devices  21.8 us (38%)
  Pallas kernels  12.5 us (22%)
  local copies, waits for them, and re-layouts  1.02 us (2%)
    pallas_call x17, Pallas kernels, call(): pl.pallas_call(body, out_shape=[jax.ShapeDtypeStruct(s, d) for s, d in ou...  12.5 us
    all_to_all x1, waiting for transfers between devices, local(): lax.all_to_all(back, ('sec', 'ep'), split_axis=0, concat_axis=0, tiled=True)  6.65 us
    ppermute x2, starting transfers between devices, local(): done += [total, lax.ppermute(send, 'tp', swap('tp', 2))]  6.01 us
    ppermute x3, waiting for transfers between devices, local(): lax.ppermute(values, 'ep', swap('ep', k))  5.71 us
    ppermute x3, starting transfers between devices, local(): lax.ppermute(values, 'ep', swap('ep', k))  5.68 us
    ppermute x2, waiting for transfers between devices, local(): done += [total, lax.ppermute(send, 'tp', swap('tp', 2))]  4.24 us
    all_to_all x1, starting transfers between devices, local(): lax.all_to_all(back, ('sec', 'ep'), split_axis=0, concat_axis=0, tiled=True)  3.62 us
    ppermute x1, waiting for transfers between devices, local(): cross = lax.ppermute(part, axes, turn(1))  2.33 us
  transfers between devices with their start and end apart: 14, of which 9 were waited for; matrix products, arithmetic and copies ran while one was open for 0% of the time, Pallas kernels for 8%

profile of v3, /device:TPU:0, one launch (start us, length us, event | category | flops | bytes accessed | tf_op | source)
XLA Modules:
  0.0 57.5 jit_solution(5100710508994523991)
XLA Ops:
  0.1 0.8 %copy-done.4 = bf16[4,16,576]{2,1,0:T(8,128)(2,1)S(1)} copy-done((bf16[4,16,576]{2,1,0:T(8,128)(2,1)S(1)}, bf16[4,16,576]{2,1,0:T(8,128)(2,1)}, u32[]{:S(2)}) %copy-start.4) | copy-done | bytes 73752
  0.9 0.1 copy-done.3
  1.0 1.0 %shard_map.119.latent = f32[4,16,512]{2,1,0:T(8,128)S(1)} custom-call(s32[4]{0:T(128)S(1)} %copy-done.6, bf16[4,16,576]{2,1,0:T(8,128)(2,1)S(1)} %copy-done.4, bf16[4,32,576]{2,1,0:T(8,128)(2,1)S(1)} %copy-done.3, bf16[64,64]{1,0:T(8,128)(2,1)S(1)} %shard_map.118.pick), custom_call_target="tpu_custom_call" | custom-call | flops 1000000000 | bytes 1000000 | tf_op jit(solution)/shard_map/pallas_call | solution.py:33
  2.0 0.0 copy-done.5
  2.0 0.0 slice-start.13
  2.0 0.0 slice-start.4
  2.0 0.0 slice-start.8
  2.0 1.0 %shard_map.120.own = bf16[16,1024]{1,0:T(8,128)(2,1)S(1)} custom-call(s32[4,4]{1,0:T(4,128)S(1)} %copy-done, f32[4,16,512]{2,1,0:T(8,128)S(1)} %shard_map.119.latent, bf16[16,512,128]{2,1,0:T(8,128)(2,1)S(1)} %copy-done.2, bf16[4,1792]{1,0:T(4,128)(2,1)S(1)} %copy-done.5), custom_call_target="tpu_custom_call" | custom-call | flops 20000000000 | bytes 1000000 | tf_op jit(solution)/shard_map/pallas_call | solution.py:33
  3.0 0.0 slice-start.5
  3.0 0.0 slice-start.6
  3.0 0.0 slice-start.7
  3.1 0.0 slice-start.9
  3.1 0.0 slice-start.10
  3.1 0.0 slice-start.11
  3.1 3.1 %collective-permute-start = (bf16[16,1024]{1,0:T(8,128)(2,1)S(1)}, bf16[16,1024]{1,0:T(8,128)(2,1)S(1)}, u32[]{:S(2)}, u32[]{:S(2)}) collective-permute-start(bf16[16,1024]{1,0:T(8,128)(2,1)S(1)} %shard_map.120.own), channel_id=1, source_target_pairs={{0,4},{4,0},{8,12},{12,8},{1,5},{5,1},{9,13},{13,9},{2,6},{6,2},{1... | collective-permute-start | bytes 98312 | tf_op jit(solution)/shard_map/ppermute | solution.py:381
  6.2 2.6 %collective-permute-start.1 = (bf16[16,1024]{1,0:T(8,128)(2,1)S(1)}, bf16[16,1024]{1,0:T(8,128)(2,1)S(1)}, u32[]{:S(2)}, u32[]{:S(2)}) collective-permute-start(bf16[16,1024]{1,0:T(8,128)(2,1)S(1)} %shard_map.120.own), channel_id=1, source_target_pairs={{0,8},{4,12},{8,0},{12,4},{1,9},{5,13},{9,1},{13,5},{2,10},{6,14},... | collective-permute-start | bytes 98312 | tf_op jit(solution)/shard_map/ppermute | solution.py:381
  8.8 0.0 collective-permute-start.2
  8.8 2.8 %collective-permute-done.1.got2 = bf16[16,1024]{1,0:T(8,128)(2,1)S(1)} collective-permute-done((bf16[16,1024]{1,0:T(8,128)(2,1)S(1)}, bf16[16,1024]{1,0:T(8,128)(2,1)S(1)}, u32[]{:S(2)}, u32[]{:S(2)}) %collective-permute-start.1) | collective-permute-done | bytes 32800 | tf_op jit(solution)/shard_map/ppermute | solution.py:381
  11.6 2.9 %collective-permute-done.2.got3 = bf16[16,1024]{1,0:T(8,128)(2,1)S(1)} collective-permute-done((bf16[16,1024]{1,0:T(8,128)(2,1)S(1)}, bf16[16,1024]{1,0:T(8,128)(2,1)S(1)}, u32[]{:S(2)}, u32[]{:S(2)}) %collective-permute-start.2) | collective-permute-done | bytes 32800 | tf_op jit(solution)/shard_map/ppermute | solution.py:381
  14.5 1.2 %shard_map.121 = (f32[16,1792]{1,0:T(8,128)S(1)}, bf16[32,1024]{1,0:T(8,128)(2,1)S(1)}) custom-call(bf16[64,64]{1,0:T(8,128)(2,1)S(1)} %shard_map.118.pick, bf16[16,1024]{1,0:T(8,128)(2,1)S(1)} %shard_map.120.own, bf16[16,1024]{1,0:T(8,128)(2,1)S(1)} %collective-permute-done.got1, bf16[16,1024]{1,0:T(8,128)(2,1)S(1)} %collective-permute-done.1.got2, ...), custom_call_target="tpu_custom_call" | custom-call | flops 60000002048 | bytes 1000000 | tf_op jit(solution)/shard_map/pallas_call | solution.py:33
  15.7 1.3 %collective-permute-done.4.two = f32[16,1792]{1,0:T(8,128)S(1)} collective-permute-done((f32[16,1792]{1,0:T(8,128)S(1)}, f32[16,1792]{1,0:T(8,128)S(1)}, u32[]{:S(2)}, u32[]{:S(2)}) %collective-permute-start.4) | collective-permute-done | bytes 114720 | tf_op jit(solution)/shard_map/ppermute | solution.py:389
  17.0 1.6 %collective-permute-start.5 = (bf16[16,1792]{1,0:T(8,128)(2,1)S(1)}, bf16[16,1792]{1,0:T(8,128)(2,1)S(1)}, u32[]{:S(2)}, u32[]{:S(2)}) collective-permute-start(bf16[16,1792]{1,0:T(8,128)(2,1)S(1)} %shard_map.123.one), channel_id=1, source_target_pairs={{0,2},{1,3},{2,0},{3,1},{4,6},{5,7},{6,4},{7,5},{8,10},{9,11},{10,... | collective-permute-start | bytes 172040 | tf_op jit(solution)/shard_map/ppermute | solution.py:392
  18.6 1.5 %collective-permute-start.3 = (bf16[32,1024]{1,0:T(8,128)(2,1)S(1)}, bf16[32,1024]{1,0:T(8,128)(2,1)S(1)}, u32[]{:S(2)}, u32[]{:S(2)}) collective-permute-start(bf16[32,1024]{1,0:T(8,128)(2,1)S(1)} %get-tuple-element.17.extra), channel_id=1, source_target_pairs={{0,16},{16,0},{1,17},{17,1},{2,18},{18,2},{3,19},{19,3},{4,20},{20... | collective-permute-start | bytes 196616 | tf_op jit(solution)/shard_map/ppermute | solution.py:390
  20.1 1.2 %collective-permute-done.5.two = bf16[16,1792]{1,0:T(8,128)(2,1)S(1)} collective-permute-done((bf16[16,1792]{1,0:T(8,128)(2,1)S(1)}, bf16[16,1792]{1,0:T(8,128)(2,1)S(1)}, u32[]{:S(2)}, u32[]{:S(2)}) %collective-permute-start.5) | collective-permute-done | bytes 57376 | tf_op jit(solution)/shard_map/ppermute | solution.py:392
  21.3 0.7 %collective-permute-start.6 = (bf16[16,1792]{1,0:T(8,128)(2,1)S(1)}, bf16[16,1792]{1,0:T(8,128)(2,1)S(1)}, u32[]{:S(2)}, u32[]{:S(2)}) collective-permute-start(bf16[16,1792]{1,0:T(8,128)(2,1)S(1)} %shard_map.124), channel_id=1, source_target_pairs={{0,0},{1,4},{2,8},{3,12},{4,1},{5,5},{6,9},{7,13},{8,2},{9,6},{10,... | collective-permute-start | bytes 172040 | tf_op jit(solution)/shard_map/ppermute | solution.py:394
  22.0 1.6 %collective-permute-start.7 = (bf16[16,1792]{1,0:T(8,128)(2,1)S(1)}, bf16[16,1792]{1,0:T(8,128)(2,1)S(1)}, u32[]{:S(2)}, u32[]{:S(2)}) collective-permute-start(bf16[16,1792]{1,0:T(8,128)(2,1)S(1)} %shard_map.124), channel_id=1, source_target_pairs={{0,16},{1,20},{2,24},{3,28},{4,17},{5,21},{6,25},{7,29},{8,18},{9,... | collective-permute-start | bytes 172040 | tf_op jit(solution)/shard_map/ppermute | solution.py:395
  23.5 0.3 shard_map.122
  23.9 2.3 %collective-permute-done.7.other = bf16[16,1792]{1,0:T(8,128)(2,1)S(1)} collective-permute-done((bf16[16,1792]{1,0:T(8,128)(2,1)S(1)}, bf16[16,1792]{1,0:T(8,128)(2,1)S(1)}, u32[]{:S(2)}, u32[]{:S(2)}) %collective-permute-start.7) | collective-permute-done | bytes 57376 | tf_op jit(solution)/shard_map/ppermute | solution.py:395
  26.3 2.1 %shard_map.125 = (f32[16,2176]{1,0:T(8,128)S(1)}, f32[16,2048]{1,0:T(8,128)S(1)}, bf16[16,1792]{1,0:T(8,128)(2,1)S(1)}, bf16[4,1792]{1,0:T(4,128)(2,1)S(1)}) custom-call(f32[32,1792]{1,0:T(8,128)S(1)} %get-tuple-element.18.known, bf16[16,1792]{1,0:T(8,128)(2,1)S(1)} %collective-permute-done.6.same, bf16[16,1792]{1,0:T(8,128)(2,1)S(1)} %collective-permute-done.7.other, ...), custom_call_target="tpu_custom_call" | custom-call | flops 20000000000 | bytes 1000000 | tf_op jit(solution)/shard_map/pallas_call | solution.py:33
  28.4 1.1 %collective-permute-start.10 = (f32[16,2048]{1,0:T(8,128)S(1)}, f32[16,2048]{1,0:T(8,128)S(1)}, u32[]{:S(2)}, u32[]{:S(2)}) collective-permute-start(f32[16,2048]{1,0:T(8,128)S(1)} %get-tuple-element.26), channel_id=1, source_target_pairs={{0,1},{1,0},{2,3},{3,2},{4,5},{5,4},{6,7},{7,6},{8,9},{9,8},{10,11... | collective-permute-start | bytes 393224 | tf_op jit(solution)/shard_map/ppermute | solution.py:415
  29.6 0.0 collective-permute-start.8
  29.6 1.1 %shard_map.126.own = f32[16,2176]{1,0:T(8,128)S(1)} custom-call(bf16[16,1792]{1,0:T(8,128)(2,1)S(1)} %get-tuple-element.22.mine, f32[1,1792]{1,0:T(1,128)S(1)} %reshape.3.gain, bf16[16,1792,256]{2,1,0:T(8,128)(2,1)S(1)} %bitcast.3, bf16[16,1792,256]{2,1,0:T(8,128)(2,1)S(1)} %bitcast.5), custom_call_target="tpu_custom_call" | custom-call | flops 20000000000 | bytes 1000000 | tf_op jit(solution)/shard_map/pallas_call | solution.py:33
  30.7 0.3 collective-permute-done.8.got
  30.9 0.1 shard_map.127
  31.0 5.9 %collective-permute-start.9 = (bf16[16,2176]{1,0:T(8,128)(2,1)S(1)}, bf16[16,2176]{1,0:T(8,128)(2,1)S(1)}, u32[]{:S(2)}, u32[]{:S(2)}) collective-permute-start(bf16[16,2176]{1,0:T(8,128)(2,1)S(1)} %get-tuple-element.25), channel_id=1, source_target_pairs={{0,2},{1,3},{2,0},{3,1},{4,6},{5,7},{6,4},{7,5},{8,10},{9,11},{10,... | collective-permute-start | bytes 208904 | tf_op jit(solution)/shard_map/ppermute | solution.py:429
  37.0 1.1 %shard_map.128.own = f32[16,2048]{1,0:T(8,128)S(1)} custom-call(bf16[16,1792]{1,0:T(8,128)(2,1)S(1)} %get-tuple-element.22.mine, f32[1,1792]{1,0:T(1,128)S(1)} %reshape.3.gain, bf16[16,1792,256]{2,1,0:T(8,128)(2,1)S(1)} %bitcast.3, bf16[16,1792,256]{2,1,0:T(8,128)(2,1)S(1)} %bitcast.5), custom_call_target="tpu_custom_call" | custom-call | flops 20000000000 | bytes 1000000 | tf_op jit(solution)/shard_map/pallas_call | solution.py:33
  38.1 0.1 collective-permute-start.11
  38.1 4.2 %collective-permute-done.11.got1 = bf16[16,2048]{1,0:T(8,128)(2,1)S(1)} collective-permute-done((bf16[16,2048]{1,0:T(8,128)(2,1)S(1)}, bf16[16,2048]{1,0:T(8,128)(2,1)S(1)}, u32[]{:S(2)}, u32[]{:S(2)}) %collective-permute-start.11) | collective-permute-done | bytes 65568 | tf_op jit(solution)/shard_map/ppermute | solution.py:429
  42.4 0.1 shard_map.130.act
  42.5 0.0 copy-start.1
  42.5 0.1 collective-permute-start.12
  42.7 1.1 %shard_map.131.done = bf16[16,1792]{1,0:T(8,128)(2,1)S(1)} custom-call(bf16[16,2048]{1,0:T(8,128)(2,1)S(1)} %shard_map.130.act, bf16[16,256,1792]{2,1,0:T(8,128)(2,1)S(1)} %bitcast.1), custom_call_target="tpu_custom_call" | custom-call | tf_op jit(solution)/shard_map/pallas_call | solution.py:33
  43.7 0.1 collective-permute-done.12.act
  43.9 1.9 %shard_map.132 = bf16[8,8,896]{2,1,0:T(8,128)(2,1)} custom-call(bf16[16,2048]{1,0:T(8,128)(2,1)S(1)} %collective-permute-done.12.act, bf16[16,256,1792]{2,1,0:T(8,128)(2,1)S(1)} %bitcast.1, bf16[16,1792]{1,0:T(8,128)(2,1)S(1)} %shard_map.131.done), custom_call_target="tpu_custom_call" | custom-call | tf_op jit(solution)/shard_map/pallas_call | solution.py:33
  45.8 3.6 %all-to-all-start = ((bf16[8,8,896]{2,1,0:T(8,128)(2,1)}), bf16[8,8,896]{2,1,0:T(8,128)(2,1)S(1)}, u32[]{:S(2)}, u32[]{:S(2)}) async-start(bf16[8,8,896]{2,1,0:T(8,128)(2,1)} %shard_map.132), calls=%async_computation | async-start | bytes 229376 | tf_op jit(solution)/shard_map/all_to_all | solution.py:439
  49.4 0.7 %shard_map.133.mix = bf16[24,64]{1,0:T(8,128)(2,1)S(1)} custom-call(s32[4,4]{1,0:T(4,128)S(1)} %copy-done, f32[4,4]{1,0:T(4,128)S(1)} %copy-done.1), custom_call_target="tpu_custom_call" | custom-call | tf_op jit(solution)/shard_map/pallas_call | solution.py:33
  50.1 6.7 %all-to-all-done.back = bf16[8,8,896]{2,1,0:T(8,128)(2,1)S(1)} async-done(((bf16[8,8,896]{2,1,0:T(8,128)(2,1)}), bf16[8,8,896]{2,1,0:T(8,128)(2,1)S(1)}, u32[]{:S(2)}, u32[]{:S(2)}) %all-to-all-start) | async-done | bytes 114720 | tf_op jit(solution)/shard_map/all_to_all | solution.py:439
  56.8 0.7 %shard_map.134 = bf16[4,1792]{1,0:T(4,128)(2,1)} custom-call(bf16[4,1792]{1,0:T(4,128)(2,1)S(1)} %get-tuple-element.21.state, bf16[8,8,896]{2,1,0:T(8,128)(2,1)S(1)} %all-to-all-done.back, bf16[24,64]{1,0:T(8,128)(2,1)S(1)} %shard_map.133.mix), custom_call_target="tpu_custom_call" | custom-call | tf_op jit(solution)/shard_map/pallas_call | solution.py:33
  (46 shorter events, 0.2 us)
Async XLA Ops:
  0.0 0.9 %copy-start.4 = (bf16[4,16,576]{2,1,0:T(8,128)(2,1)S(1)}, bf16[4,16,576]{2,1,0:T(8,128)(2,1)}, u32[]{:S(2)}) copy-start(bf16[4,16,576]{2,1,0:T(8,128)(2,1)} %queries.1) | copy-start | bytes 221188
  0.0 1.0 %copy-start.3 = (bf16[4,32,576]{2,1,0:T(8,128)(2,1)S(1)}, bf16[4,32,576]{2,1,0:T(8,128)(2,1)}, u32[]{:S(2)}) copy-start(bf16[4,32,576]{2,1,0:T(8,128)(2,1)} %cache.1) | copy-start | bytes 442372
  0.0 1.0 %copy-start.6 = (s32[4]{0:T(128)S(1)}, s32[4]{0:T(128)}, u32[]{:S(2)}) copy-start(s32[4]{0:T(128)} %lengths.1) | copy-start | bytes 52
  0.0 1.9 %copy-start.2 = (bf16[16,512,128]{2,1,0:T(8,128)(2,1)S(1)}, bf16[16,512,128]{2,1,0:T(8,128)(2,1)}, u32[]{:S(2)}) copy-start(bf16[16,512,128]{2,1,0:T(8,128)(2,1)} %w_uv.1) | copy-start | bytes 6291460
  0.0 2.0 %copy-start.5 = (bf16[4,1792]{1,0:T(4,128)(2,1)S(1)}, bf16[4,1792]{1,0:T(4,128)(2,1)}, u32[]{:S(2)}) copy-start(bf16[4,1792]{1,0:T(4,128)(2,1)} %residual.1) | copy-start | bytes 43012
  0.0 2.0 %copy-start = (s32[4,4]{1,0:T(4,128)S(1)}, s32[4,4]{1,0:T(4,128)}, u32[]{:S(2)}) copy-start(s32[4,4]{1,0:T(4,128)} %ids.3) | copy-start | bytes 196
  1.0 13.5 %slice-start.12 = ((s8[7340032]{0:T(1024)(128)(4,1)}), s8[4194304]{0:T(1024)(128)(4,1)S(1)}, s32[]{:S(2)}) async-start(s8[7340032]{0:T(1024)(128)(4,1)} %bitcast.6), calls=%async_computation.13 | async-start | bytes 8388608
  2.0 12.5 %slice-start.13 = ((s8[7340032]{0:T(1024)(128)(4,1)}), s8[3145728]{0:T(1024)(128)(4,1)S(1)}, s32[]{:S(2)}) async-start(s8[7340032]{0:T(1024)(128)(4,1)} %bitcast.6), calls=%async_computation.14 | async-start | bytes 6291456
  2.0 24.2 %slice-start.4 = ((s8[14680064]{0:T(1024)(128)(4,1)}), s8[4194304]{0:T(1024)(128)(4,1)S(1)}, s32[]{:S(2)}) async-start(s8[14680064]{0:T(1024)(128)(4,1)} %bitcast.2), calls=%async_computation.5 | async-start | bytes 8388608
  2.0 24.2 %slice-start.8 = ((s8[14680064]{0:T(1024)(128)(4,1)}), s8[4194304]{0:T(1024)(128)(4,1)S(1)}, s32[]{:S(2)}) async-start(s8[14680064]{0:T(1024)(128)(4,1)} %bitcast.4), calls=%async_computation.9 | async-start | bytes 8388608
  3.0 20.5 %copy-start.7 = (f32[1792]{0:T(1024)S(1)}, f32[1792]{0:T(1024)}, u32[]{:S(2)}) copy-start(f32[1792]{0:T(1024)} %param.18) | copy-start | bytes 21508
  3.0 23.2 %slice-start.5 = ((s8[14680064]{0:T(1024)(128)(4,1)}), s8[4194304]{0:T(1024)(128)(4,1)S(1)}, s32[]{:S(2)}) async-start(s8[14680064]{0:T(1024)(128)(4,1)} %bitcast.2), calls=%async_computation.6 | async-start | bytes 8388608
  3.0 23.2 %slice-start.6 = ((s8[14680064]{0:T(1024)(128)(4,1)}), s8[4194304]{0:T(1024)(128)(4,1)S(1)}, s32[]{:S(2)}) async-start(s8[14680064]{0:T(1024)(128)(4,1)} %bitcast.2), calls=%async_computation.7 | async-start | bytes 8388608
  3.0 23.2 %slice-start.7 = ((s8[14680064]{0:T(1024)(128)(4,1)}), s8[2097152]{0:T(1024)(128)(4,1)S(1)}, s32[]{:S(2)}) async-start(s8[14680064]{0:T(1024)(128)(4,1)} %bitcast.2), calls=%async_computation.8 | async-start | bytes 4194304
  3.1 23.2 %slice-start.9 = ((s8[14680064]{0:T(1024)(128)(4,1)}), s8[4194304]{0:T(1024)(128)(4,1)S(1)}, s32[]{:S(2)}) async-start(s8[14680064]{0:T(1024)(128)(4,1)} %bitcast.4), calls=%async_computation.10 | async-start | bytes 8388608
  3.1 23.2 %slice-start.10 = ((s8[14680064]{0:T(1024)(128)(4,1)}), s8[4194304]{0:T(1024)(128)(4,1)S(1)}, s32[]{:S(2)}) async-start(s8[14680064]{0:T(1024)(128)(4,1)} %bitcast.4), calls=%async_computation.11 | async-start | bytes 8388608
  3.1 23.2 %slice-start.11 = ((s8[14680064]{0:T(1024)(128)(4,1)}), s8[2097152]{0:T(1024)(128)(4,1)S(1)}, s32[]{:S(2)}) async-start(s8[14680064]{0:T(1024)(128)(4,1)} %bitcast.4), calls=%async_computation.12 | async-start | bytes 4194304
  3.1 5.7 %collective-permute-start = (bf16[16,1024]{1,0:T(8,128)(2,1)S(1)}, bf16[16,1024]{1,0:T(8,128)(2,1)S(1)}, u32[]{:S(2)}, u32[]{:S(2)}) collective-permute-start(bf16[16,1024]{1,0:T(8,128)(2,1)S(1)} %shard_map.120.own), channel_id=1, source_target_pairs={{0,4},{4,0},{8,12},{12,8},{1,5},{5,1},{9,13},{13,9},{2,6},{6,2},{1... | collective-permute-start | bytes 98312 | tf_op jit(solution)/shard_map/ppermute | solution.py:381
  6.2 5.4 %collective-permute-start.1 = (bf16[16,1024]{1,0:T(8,128)(2,1)S(1)}, bf16[16,1024]{1,0:T(8,128)(2,1)S(1)}, u32[]{:S(2)}, u32[]{:S(2)}) collective-permute-start(bf16[16,1024]{1,0:T(8,128)(2,1)S(1)} %shard_map.120.own), channel_id=1, source_target_pairs={{0,8},{4,12},{8,0},{12,4},{1,9},{5,13},{9,1},{13,5},{2,10},{6,14},... | collective-permute-start | bytes 98312 | tf_op jit(solution)/shard_map/ppermute | solution.py:381
  8.8 5.7 %collective-permute-start.2 = (bf16[16,1024]{1,0:T(8,128)(2,1)S(1)}, bf16[16,1024]{1,0:T(8,128)(2,1)S(1)}, u32[]{:S(2)}, u32[]{:S(2)}) collective-permute-start(bf16[16,1024]{1,0:T(8,128)(2,1)S(1)} %shard_map.120.own), channel_id=1, source_target_pairs={{0,12},{4,8},{8,4},{12,0},{1,13},{5,9},{9,5},{13,1},{2,14},{6,10},... | collective-permute-start | bytes 98312 | tf_op jit(solution)/shard_map/ppermute | solution.py:381
  15.7 1.3 %collective-permute-start.4 = (f32[16,1792]{1,0:T(8,128)S(1)}, f32[16,1792]{1,0:T(8,128)S(1)}, u32[]{:S(2)}, u32[]{:S(2)}) collective-permute-start(f32[16,1792]{1,0:T(8,128)S(1)} %get-tuple-element.19.one), channel_id=1, source_target_pairs={{0,1},{1,0},{2,3},{3,2},{4,5},{5,4},{6,7},{7,6},{8,9},{9,8},{10,11... | collective-permute-start | bytes 344072 | tf_op jit(solution)/shard_map/ppermute | solution.py:389
  17.0 4.2 %collective-permute-start.5 = (bf16[16,1792]{1,0:T(8,128)(2,1)S(1)}, bf16[16,1792]{1,0:T(8,128)(2,1)S(1)}, u32[]{:S(2)}, u32[]{:S(2)}) collective-permute-start(bf16[16,1792]{1,0:T(8,128)(2,1)S(1)} %shard_map.123.one), channel_id=1, source_target_pairs={{0,2},{1,3},{2,0},{3,1},{4,6},{5,7},{6,4},{7,5},{8,10},{9,11},{10,... | collective-permute-start | bytes 172040 | tf_op jit(solution)/shard_map/ppermute | solution.py:392
  18.6 4.9 %collective-permute-start.3 = (bf16[32,1024]{1,0:T(8,128)(2,1)S(1)}, bf16[32,1024]{1,0:T(8,128)(2,1)S(1)}, u32[]{:S(2)}, u32[]{:S(2)}) collective-permute-start(bf16[32,1024]{1,0:T(8,128)(2,1)S(1)} %get-tuple-element.17.extra), channel_id=1, source_target_pairs={{0,16},{16,0},{1,17},{17,1},{2,18},{18,2},{3,19},{19,3},{4,20},{20... | collective-permute-start | bytes 196616 | tf_op jit(solution)/shard_map/ppermute | solution.py:390
  21.3 2.6 %collective-permute-start.6 = (bf16[16,1792]{1,0:T(8,128)(2,1)S(1)}, bf16[16,1792]{1,0:T(8,128)(2,1)S(1)}, u32[]{:S(2)}, u32[]{:S(2)}) collective-permute-start(bf16[16,1792]{1,0:T(8,128)(2,1)S(1)} %shard_map.124), channel_id=1, source_target_pairs={{0,0},{1,4},{2,8},{3,12},{4,1},{5,5},{6,9},{7,13},{8,2},{9,6},{10,... | collective-permute-start | bytes 172040 | tf_op jit(solution)/shard_map/ppermute | solution.py:394
  22.0 4.2 %collective-permute-start.7 = (bf16[16,1792]{1,0:T(8,128)(2,1)S(1)}, bf16[16,1792]{1,0:T(8,128)(2,1)S(1)}, u32[]{:S(2)}, u32[]{:S(2)}) collective-permute-start(bf16[16,1792]{1,0:T(8,128)(2,1)S(1)} %shard_map.124), channel_id=1, source_target_pairs={{0,16},{1,20},{2,24},{3,28},{4,17},{5,21},{6,25},{7,29},{8,18},{9,... | collective-permute-start | bytes 172040 | tf_op jit(solution)/shard_map/ppermute | solution.py:395
  28.4 9.6 %collective-permute-start.10 = (f32[16,2048]{1,0:T(8,128)S(1)}, f32[16,2048]{1,0:T(8,128)S(1)}, u32[]{:S(2)}, u32[]{:S(2)}) collective-permute-start(f32[16,2048]{1,0:T(8,128)S(1)} %get-tuple-element.26), channel_id=1, source_target_pairs={{0,1},{1,0},{2,3},{3,2},{4,5},{5,4},{6,7},{7,6},{8,9},{9,8},{10,11... | collective-permute-start | bytes 393224 | tf_op jit(solution)/shard_map/ppermute | solution.py:415
  29.6 1.4 %collective-permute-start.8 = (f32[16,2176]{1,0:T(8,128)S(1)}, f32[16,2176]{1,0:T(8,128)S(1)}, u32[]{:S(2)}, u32[]{:S(2)}) collective-permute-start(f32[16,2176]{1,0:T(8,128)S(1)} %get-tuple-element.23), channel_id=1, source_target_pairs={{0,1},{1,0},{2,3},{3,2},{4,5},{5,4},{6,7},{7,6},{8,9},{9,8},{10,11... | collective-permute-start | bytes 417800 | tf_op jit(solution)/shard_map/ppermute | solution.py:415
  31.0 11.6 %slice-start = ((s8[14680064]{0:T(1024)(128)(4,1)}), s8[4194304]{0:T(1024)(128)(4,1)S(1)}, s32[]{:S(2)}) async-start(s8[14680064]{0:T(1024)(128)(4,1)} %bitcast), calls=%async_computation.1 | async-start | bytes 8388608
  31.0 11.6 %slice-start.1 = ((s8[14680064]{0:T(1024)(128)(4,1)}), s8[4194304]{0:T(1024)(128)(4,1)S(1)}, s32[]{:S(2)}) async-start(s8[14680064]{0:T(1024)(128)(4,1)} %bitcast), calls=%async_computation.2 | async-start | bytes 8388608
  31.0 11.6 %slice-start.2 = ((s8[14680064]{0:T(1024)(128)(4,1)}), s8[4194304]{0:T(1024)(128)(4,1)S(1)}, s32[]{:S(2)}) async-start(s8[14680064]{0:T(1024)(128)(4,1)} %bitcast), calls=%async_computation.3 | async-start | bytes 8388608
  31.0 11.6 %slice-start.3 = ((s8[14680064]{0:T(1024)(128)(4,1)}), s8[2097152]{0:T(1024)(128)(4,1)S(1)}, s32[]{:S(2)}) async-start(s8[14680064]{0:T(1024)(128)(4,1)} %bitcast), calls=%async_computation.4 | async-start | bytes 4194304
  31.0 11.4 %collective-permute-start.9 = (bf16[16,2176]{1,0:T(8,128)(2,1)S(1)}, bf16[16,2176]{1,0:T(8,128)(2,1)S(1)}, u32[]{:S(2)}, u32[]{:S(2)}) collective-permute-start(bf16[16,2176]{1,0:T(8,128)(2,1)S(1)} %get-tuple-element.25), channel_id=1, source_target_pairs={{0,2},{1,3},{2,0},{3,1},{4,6},{5,7},{6,4},{7,5},{8,10},{9,11},{10,... | collective-permute-start | bytes 208904 | tf_op jit(solution)/shard_map/ppermute | solution.py:429
  38.1 4.3 %collective-permute-start.11 = (bf16[16,2048]{1,0:T(8,128)(2,1)S(1)}, bf16[16,2048]{1,0:T(8,128)(2,1)S(1)}, u32[]{:S(2)}, u32[]{:S(2)}) collective-permute-start(bf16[16,2048]{1,0:T(8,128)(2,1)S(1)} %get-tuple-element.28), channel_id=1, source_target_pairs={{0,2},{1,3},{2,0},{3,1},{4,6},{5,7},{6,4},{7,5},{8,10},{9,11},{10,... | collective-permute-start | bytes 196616 | tf_op jit(solution)/shard_map/ppermute | solution.py:429
  42.5 6.9 %copy-start.1 = (f32[4,4]{1,0:T(4,128)S(1)}, f32[4,4]{1,0:T(4,128)}, u32[]{:S(2)}) copy-start(f32[4,4]{1,0:T(4,128)} %weights.1) | copy-start | bytes 196
  42.5 1.3 %collective-permute-start.12 = (bf16[16,2048]{1,0:T(8,128)(2,1)S(1)}, bf16[16,2048]{1,0:T(8,128)(2,1)S(1)}, u32[]{:S(2)}, u32[]{:S(2)}) collective-permute-start(bf16[16,2048]{1,0:T(8,128)(2,1)S(1)} %shard_map.130.act), channel_id=1, source_target_pairs={{0,1},{1,0},{2,3},{3,2},{4,5},{5,4},{6,7},{7,6},{8,9},{9,8},{10,11... | collective-permute-start | bytes 196616 | tf_op jit(solution)/shard_map/ppermute | solution.py:431
  45.8 11.0 %all-to-all-start = ((bf16[8,8,896]{2,1,0:T(8,128)(2,1)}), bf16[8,8,896]{2,1,0:T(8,128)(2,1)S(1)}, u32[]{:S(2)}, u32[]{:S(2)}) async-start(bf16[8,8,896]{2,1,0:T(8,128)(2,1)} %shard_map.132), calls=%async_computation | async-start | bytes 229376 | tf_op jit(solution)/shard_map/all_to_all | solution.py:439

commit v4 on v3

--- a/solution.py
+++ b/solution.py
@@ -127,7 +127,8 @@
     out[...] = (one[...].astype(f32) + two[...].astype(f32)).astype(bf16)
 
 
-def choose_body(extra, got, known, choice):
+def choose_body(extra, got, ids, weights, known, choice, mix):
+    write_mix(ids, weights, mix)
     me, sec = lax.axis_index("ep"), lax.axis_index("sec")
     block = extra.shape[0] // 2
     rows = block // 4
@@ -172,7 +173,7 @@
     )
 
 
-def mix_body(ids, weights, mix):
+def write_mix(ids, weights, mix):
     rows, top = ids.shape
     slots = []
     for r in range(rows):
@@ -393,14 +394,15 @@
     (part,) = call(add_body, [((ep * rows, columns), bf16)], (part, got), [VMEM] * 2, cost=COSTS[5])
     same = lax.ppermute(part, axes, turn(0))
     cross = lax.ppermute(part, axes, turn(1))
-    known, choice = call(
+    known, choice, mix = call(
         choose_body,
-        [((groups * rows, columns), f32), ((2 * lines + 8, groups * rows), bf16)],
-        (extra, beyond),
-        [VMEM] * 2,
-    )
-    (mix,) = call(
-        mix_body, [((6 * rows, groups * 2 * slots), bf16)], (expert_ids, expert_weights), [SMEM] * 2
+        [
+            ((groups * rows, columns), f32),
+            ((2 * lines + 8, groups * rows), bf16),
+            ((6 * rows, groups * 2 * slots), bf16),
+        ],
+        (extra, beyond, expert_ids, expert_weights),
+        [VMEM, VMEM, SMEM, SMEM],
     )
     wides = (hidden + 128, hidden)
     away0, away1, mine, state = call(

time: 57.8 us -> 56.9 us (0.984)
  blocking collectives: 0 us -> 10.8 us
  waiting for transfers between devices: 21.8 us -> 14.6 us
  starting transfers between devices: 21.8 us -> 18.2 us
  Pallas kernels: 12.5 us -> 11.7 us
    all_to_all x0 -> x1, blocking collectives: none -> 10.8 us  [local(): lax.all_to_all(back, ('sec', 'ep'), split_axis=0, concat_axis=0, tiled=True)]
    all_to_all x1 -> x0, waiting for transfers between devices: 6.65 us -> none  [local(): lax.all_to_all(back, ('sec', 'ep'), split_axis=0, concat_axis=0, tiled=True)]
    all_to_all x1 -> x0, starting transfers between devices: 3.62 us -> none  [local(): lax.all_to_all(back, ('sec', 'ep'), split_axis=0, concat_axis=0, tiled=True)]
    pallas_call x17 -> x16, Pallas kernels: 12.5 us -> 11.7 us  [call(): pl.pallas_call(body, out_shape=[jax.ShapeDtypeStruct(s, d) for s, d in ou...]
    ppermute x1, waiting for transfers between devices: 2.33 us -> 1.72 us  [local(): cross = lax.ppermute(part, axes, turn(1))]
  transfers between devices with their start and end apart: 14 -> 13, of which waited for: 9 -> 8; matrix products, arithmetic and copies ran while one was open for 0% -> 0% of each run, Pallas kernels for 8% -> 8%
where the time goes in v4:
time: 56.9 us; the launch traced here: 56.7 us
  starting transfers between devices  18.2 us (32%)
  waiting for transfers between devices  14.6 us (26%)
  Pallas kernels  11.7 us (21%)
  blocking collectives  10.8 us (19%)
  local copies, waits for them, and re-layouts  1.02 us (2%)
    pallas_call x16, Pallas kernels, call(): pl.pallas_call(body, out_shape=[jax.ShapeDtypeStruct(s, d) for s, d in ou...  11.7 us
    all_to_all x1, blocking collectives, local(): lax.all_to_all(back, ('sec', 'ep'), split_axis=0, concat_axis=0, tiled=True)  10.8 us
    ppermute x2, starting transfers between devices, local(): done += [total, lax.ppermute(send, 'tp', swap('tp', 2))]  6.01 us
    ppermute x3, waiting for transfers between devices, local(): lax.ppermute(values, 'ep', swap('ep', k))  5.71 us
    ppermute x3, starting transfers between devices, local(): lax.ppermute(values, 'ep', swap('ep', k))  5.68 us
    ppermute x2, waiting for transfers between devices, local(): done += [total, lax.ppermute(send, 'tp', swap('tp', 2))]  4.24 us
    ppermute x1, waiting for transfers between devices, local(): cross = lax.ppermute(part, axes, turn(1))  1.72 us
    ppermute x1, starting transfers between devices, local(): got = lax.ppermute(part, 'tp', swap('tp', 2))  1.58 us
  transfers between devices with their start and end apart: 13, of which 8 were waited for; matrix products, arithmetic and copies ran while one was open for 0% of the time, Pallas kernels for 8%

profile of v4, /device:TPU:0, one launch (start us, length us, event | category | flops | bytes accessed | tf_op | source)
XLA Modules:
  0.0 56.7 jit_solution(3198788103367695401)
XLA Ops:
  0.1 0.8 %copy-done.4 = bf16[4,16,576]{2,1,0:T(8,128)(2,1)S(1)} copy-done((bf16[4,16,576]{2,1,0:T(8,128)(2,1)S(1)}, bf16[4,16,576]{2,1,0:T(8,128)(2,1)}, u32[]{:S(2)}) %copy-start.4) | copy-done | bytes 73752
  0.9 0.1 copy-done.3
  1.0 1.0 %shard_map.119.latent = f32[4,16,512]{2,1,0:T(8,128)S(1)} custom-call(s32[4]{0:T(128)S(1)} %copy-done.6, bf16[4,16,576]{2,1,0:T(8,128)(2,1)S(1)} %copy-done.4, bf16[4,32,576]{2,1,0:T(8,128)(2,1)S(1)} %copy-done.3, bf16[64,64]{1,0:T(8,128)(2,1)S(1)} %shard_map.118.pick), custom_call_target="tpu_custom_call" | custom-call | flops 1000000000 | bytes 1000000 | tf_op jit(solution)/shard_map/pallas_call | solution.py:33
  2.0 0.0 copy-done.5
  2.0 0.0 slice-start.13
  2.0 0.0 slice-start.4
  2.0 0.0 slice-start.8
  2.0 1.0 %shard_map.120.own = bf16[16,1024]{1,0:T(8,128)(2,1)S(1)} custom-call(s32[4,4]{1,0:T(4,128)S(1)} %copy-done, f32[4,16,512]{2,1,0:T(8,128)S(1)} %shard_map.119.latent, bf16[16,512,128]{2,1,0:T(8,128)(2,1)S(1)} %copy-done.2, bf16[4,1792]{1,0:T(4,128)(2,1)S(1)} %copy-done.5), custom_call_target="tpu_custom_call" | custom-call | flops 20000000000 | bytes 1000000 | tf_op jit(solution)/shard_map/pallas_call | solution.py:33
  3.0 0.0 copy-start.1
  3.0 0.0 slice-start.5
  3.1 0.0 slice-start.6
  3.1 0.0 slice-start.9
  3.1 0.0 slice-start.10
  3.1 3.1 %collective-permute-start = (bf16[16,1024]{1,0:T(8,128)(2,1)S(1)}, bf16[16,1024]{1,0:T(8,128)(2,1)S(1)}, u32[]{:S(2)}, u32[]{:S(2)}) collective-permute-start(bf16[16,1024]{1,0:T(8,128)(2,1)S(1)} %shard_map.120.own), channel_id=1, source_target_pairs={{0,4},{4,0},{8,12},{12,8},{1,5},{5,1},{9,13},{13,9},{2,6},{6,2},{1... | collective-permute-start | bytes 98312 | tf_op jit(solution)/shard_map/ppermute | solution.py:382
  6.2 2.6 %collective-permute-start.1 = (bf16[16,1024]{1,0:T(8,128)(2,1)S(1)}, bf16[16,1024]{1,0:T(8,128)(2,1)S(1)}, u32[]{:S(2)}, u32[]{:S(2)}) collective-permute-start(bf16[16,1024]{1,0:T(8,128)(2,1)S(1)} %shard_map.120.own), channel_id=1, source_target_pairs={{0,8},{4,12},{8,0},{12,4},{1,9},{5,13},{9,1},{13,5},{2,10},{6,14},... | collective-permute-start | bytes 98312 | tf_op jit(solution)/shard_map/ppermute | solution.py:382
  8.8 0.0 collective-permute-start.2
  8.8 0.0 collective-permute-done.got1
  8.8 2.8 %collective-permute-done.1.got2 = bf16[16,1024]{1,0:T(8,128)(2,1)S(1)} collective-permute-done((bf16[16,1024]{1,0:T(8,128)(2,1)S(1)}, bf16[16,1024]{1,0:T(8,128)(2,1)S(1)}, u32[]{:S(2)}, u32[]{:S(2)}) %collective-permute-start.1) | collective-permute-done | bytes 32800 | tf_op jit(solution)/shard_map/ppermute | solution.py:382
  11.6 2.9 %collective-permute-done.2.got3 = bf16[16,1024]{1,0:T(8,128)(2,1)S(1)} collective-permute-done((bf16[16,1024]{1,0:T(8,128)(2,1)S(1)}, bf16[16,1024]{1,0:T(8,128)(2,1)S(1)}, u32[]{:S(2)}, u32[]{:S(2)}) %collective-permute-start.2) | collective-permute-done | bytes 32800 | tf_op jit(solution)/shard_map/ppermute | solution.py:382
  14.5 1.2 %shard_map.121 = (f32[16,1792]{1,0:T(8,128)S(1)}, bf16[32,1024]{1,0:T(8,128)(2,1)S(1)}) custom-call(bf16[64,64]{1,0:T(8,128)(2,1)S(1)} %shard_map.118.pick, bf16[16,1024]{1,0:T(8,128)(2,1)S(1)} %shard_map.120.own, bf16[16,1024]{1,0:T(8,128)(2,1)S(1)} %collective-permute-done.got1, bf16[16,1024]{1,0:T(8,128)(2,1)S(1)} %collective-permute-done.1.got2, ...), custom_call_target="tpu_custom_call" | custom-call | flops 60000002048 | bytes 1000000 | tf_op jit(solution)/shard_map/pallas_call | solution.py:33
  15.7 1.3 %collective-permute-done.4.two = f32[16,1792]{1,0:T(8,128)S(1)} collective-permute-done((f32[16,1792]{1,0:T(8,128)S(1)}, f32[16,1792]{1,0:T(8,128)S(1)}, u32[]{:S(2)}, u32[]{:S(2)}) %collective-permute-start.4) | collective-permute-done | bytes 114720 | tf_op jit(solution)/shard_map/ppermute | solution.py:390
  17.0 1.6 %collective-permute-start.5 = (bf16[16,1792]{1,0:T(8,128)(2,1)S(1)}, bf16[16,1792]{1,0:T(8,128)(2,1)S(1)}, u32[]{:S(2)}, u32[]{:S(2)}) collective-permute-start(bf16[16,1792]{1,0:T(8,128)(2,1)S(1)} %shard_map.123.one), channel_id=1, source_target_pairs={{0,2},{1,3},{2,0},{3,1},{4,6},{5,7},{6,4},{7,5},{8,10},{9,11},{10,... | collective-permute-start | bytes 172040 | tf_op jit(solution)/shard_map/ppermute | solution.py:393
  18.6 1.5 %collective-permute-start.3 = (bf16[32,1024]{1,0:T(8,128)(2,1)S(1)}, bf16[32,1024]{1,0:T(8,128)(2,1)S(1)}, u32[]{:S(2)}, u32[]{:S(2)}) collective-permute-start(bf16[32,1024]{1,0:T(8,128)(2,1)S(1)} %get-tuple-element.18.extra), channel_id=1, source_target_pairs={{0,16},{16,0},{1,17},{17,1},{2,18},{18,2},{3,19},{19,3},{4,20},{20... | collective-permute-start | bytes 196616 | tf_op jit(solution)/shard_map/ppermute | solution.py:391
  20.1 1.2 %collective-permute-done.5.two = bf16[16,1792]{1,0:T(8,128)(2,1)S(1)} collective-permute-done((bf16[16,1792]{1,0:T(8,128)(2,1)S(1)}, bf16[16,1792]{1,0:T(8,128)(2,1)S(1)}, u32[]{:S(2)}, u32[]{:S(2)}) %collective-permute-start.5) | collective-permute-done | bytes 57376 | tf_op jit(solution)/shard_map/ppermute | solution.py:393
  21.3 0.7 %collective-permute-start.6 = (bf16[16,1792]{1,0:T(8,128)(2,1)S(1)}, bf16[16,1792]{1,0:T(8,128)(2,1)S(1)}, u32[]{:S(2)}, u32[]{:S(2)}) collective-permute-start(bf16[16,1792]{1,0:T(8,128)(2,1)S(1)} %shard_map.124), channel_id=1, source_target_pairs={{0,0},{1,4},{2,8},{3,12},{4,1},{5,5},{6,9},{7,13},{8,2},{9,6},{10,... | collective-permute-start | bytes 172040 | tf_op jit(solution)/shard_map/ppermute | solution.py:395
  22.0 1.6 %collective-permute-start.7 = (bf16[16,1792]{1,0:T(8,128)(2,1)S(1)}, bf16[16,1792]{1,0:T(8,128)(2,1)S(1)}, u32[]{:S(2)}, u32[]{:S(2)}) collective-permute-start(bf16[16,1792]{1,0:T(8,128)(2,1)S(1)} %shard_map.124), channel_id=1, source_target_pairs={{0,16},{1,20},{2,24},{3,28},{4,17},{5,21},{6,25},{7,29},{8,18},{9,... | collective-permute-start | bytes 172040 | tf_op jit(solution)/shard_map/ppermute | solution.py:396
  23.5 0.0 collective-permute-done.3.got
  23.6 0.9 %shard_map.122 = (f32[32,1792]{1,0:T(8,128)S(1)}, bf16[40,32]{1,0:T(8,128)(2,1)S(1)}, bf16[24,64]{1,0:T(8,128)(2,1)S(1)}) custom-call(bf16[32,1024]{1,0:T(8,128)(2,1)S(1)} %get-tuple-element.18.extra, bf16[32,1024]{1,0:T(8,128)(2,1)S(1)} %collective-permute-done.3.got, s32[4,4]{1,0:T(4,128)S(1)} %copy-done, f32[4,4]{1,0:T(4,128)S(1)} %copy-done.1), custom_call_target="tpu_custom_call" | custom-call | tf_op jit(solution)/shard_map/pallas_call | solution.py:33
  24.5 0.0 collective-permute-done.6.same
  24.5 1.7 %collective-permute-done.7.other = bf16[16,1792]{1,0:T(8,128)(2,1)S(1)} collective-permute-done((bf16[16,1792]{1,0:T(8,128)(2,1)S(1)}, bf16[16,1792]{1,0:T(8,128)(2,1)S(1)}, u32[]{:S(2)}, u32[]{:S(2)}) %collective-permute-start.7) | collective-permute-done | bytes 57376 | tf_op jit(solution)/shard_map/ppermute | solution.py:396
  26.3 2.1 %shard_map.125 = (f32[16,2176]{1,0:T(8,128)S(1)}, f32[16,2048]{1,0:T(8,128)S(1)}, bf16[16,1792]{1,0:T(8,128)(2,1)S(1)}, bf16[4,1792]{1,0:T(4,128)(2,1)S(1)}) custom-call(f32[32,1792]{1,0:T(8,128)S(1)} %get-tuple-element.19.known, bf16[16,1792]{1,0:T(8,128)(2,1)S(1)} %collective-permute-done.6.same, bf16[16,1792]{1,0:T(8,128)(2,1)S(1)} %collective-permute-done.7.other, ...), custom_call_target="tpu_custom_call" | custom-call | flops 20000000000 | bytes 1000000 | tf_op jit(solution)/shard_map/pallas_call | solution.py:33
  28.4 1.1 %collective-permute-start.10 = (f32[16,2048]{1,0:T(8,128)S(1)}, f32[16,2048]{1,0:T(8,128)S(1)}, u32[]{:S(2)}, u32[]{:S(2)}) collective-permute-start(f32[16,2048]{1,0:T(8,128)S(1)} %get-tuple-element.27), channel_id=1, source_target_pairs={{0,1},{1,0},{2,3},{3,2},{4,5},{5,4},{6,7},{7,6},{8,9},{9,8},{10,11... | collective-permute-start | bytes 393224 | tf_op jit(solution)/shard_map/ppermute | solution.py:417
  29.6 0.0 collective-permute-start.8
  29.6 1.1 %shard_map.126.own = f32[16,2176]{1,0:T(8,128)S(1)} custom-call(bf16[16,1792]{1,0:T(8,128)(2,1)S(1)} %get-tuple-element.23.mine, f32[1,1792]{1,0:T(1,128)S(1)} %reshape.3.gain, bf16[16,1792,256]{2,1,0:T(8,128)(2,1)S(1)} %bitcast.3, bf16[16,1792,256]{2,1,0:T(8,128)(2,1)S(1)} %bitcast.5), custom_call_target="tpu_custom_call" | custom-call | flops 20000000000 | bytes 1000000 | tf_op jit(solution)/shard_map/pallas_call | solution.py:33
  30.7 0.3 collective-permute-done.8.got
  30.9 0.1 shard_map.127
  31.0 0.0 slice-start.3
  31.0 5.9 %collective-permute-start.9 = (bf16[16,2176]{1,0:T(8,128)(2,1)S(1)}, bf16[16,2176]{1,0:T(8,128)(2,1)S(1)}, u32[]{:S(2)}, u32[]{:S(2)}) collective-permute-start(bf16[16,2176]{1,0:T(8,128)(2,1)S(1)} %get-tuple-element.26), channel_id=1, source_target_pairs={{0,2},{1,3},{2,0},{3,1},{4,6},{5,7},{6,4},{7,5},{8,10},{9,11},{10,... | collective-permute-start | bytes 208904 | tf_op jit(solution)/shard_map/ppermute | solution.py:431
  37.0 1.1 %shard_map.128.own = f32[16,2048]{1,0:T(8,128)S(1)} custom-call(bf16[16,1792]{1,0:T(8,128)(2,1)S(1)} %get-tuple-element.23.mine, f32[1,1792]{1,0:T(1,128)S(1)} %reshape.3.gain, bf16[16,1792,256]{2,1,0:T(8,128)(2,1)S(1)} %bitcast.3, bf16[16,1792,256]{2,1,0:T(8,128)(2,1)S(1)} %bitcast.5), custom_call_target="tpu_custom_call" | custom-call | flops 20000000000 | bytes 1000000 | tf_op jit(solution)/shard_map/pallas_call | solution.py:33
  38.1 0.1 collective-permute-start.11
  38.2 4.2 %collective-permute-done.11.got1 = bf16[16,2048]{1,0:T(8,128)(2,1)S(1)} collective-permute-done((bf16[16,2048]{1,0:T(8,128)(2,1)S(1)}, bf16[16,2048]{1,0:T(8,128)(2,1)S(1)}, u32[]{:S(2)}, u32[]{:S(2)}) %collective-permute-start.11) | collective-permute-done | bytes 65568 | tf_op jit(solution)/shard_map/ppermute | solution.py:431
  42.4 0.1 shard_map.130.act
  42.5 0.1 collective-permute-start.12
  42.7 1.1 %shard_map.131.done = bf16[16,1792]{1,0:T(8,128)(2,1)S(1)} custom-call(bf16[16,2048]{1,0:T(8,128)(2,1)S(1)} %shard_map.130.act, bf16[16,256,1792]{2,1,0:T(8,128)(2,1)S(1)} %bitcast.1), custom_call_target="tpu_custom_call" | custom-call | tf_op jit(solution)/shard_map/pallas_call | solution.py:33
  43.7 0.1 collective-permute-done.12.act
  43.9 1.2 %shard_map.132 = bf16[8,8,896]{2,1,0:T(8,128)(2,1)S(1)} custom-call(bf16[16,2048]{1,0:T(8,128)(2,1)S(1)} %collective-permute-done.12.act, bf16[16,256,1792]{2,1,0:T(8,128)(2,1)S(1)} %bitcast.1, bf16[16,1792]{1,0:T(8,128)(2,1)S(1)} %shard_map.131.done), custom_call_target="tpu_custom_call" | custom-call | tf_op jit(solution)/shard_map/pallas_call | solution.py:33
  45.1 10.8 %all_to_all.5.back = bf16[8,8,896]{2,1,0:T(8,128)(2,1)S(1)} all-to-all(bf16[8,8,896]{2,1,0:T(8,128)(2,1)S(1)} %shard_map.132), channel_id=1, replica_groups=mesh['sec'=2,'ep'=4,'tp'=4] {'sec','ep'}, dimensions={0} | all-to-all | bytes 229376 | tf_op jit(solution)/shard_map/all_to_all | solution.py:441
  55.9 0.7 %shard_map.133 = bf16[4,1792]{1,0:T(4,128)(2,1)} custom-call(bf16[4,1792]{1,0:T(4,128)(2,1)S(1)} %get-tuple-element.22.state, bf16[8,8,896]{2,1,0:T(8,128)(2,1)S(1)} %all_to_all.5.back, bf16[24,64]{1,0:T(8,128)(2,1)S(1)} %get-tuple-element.30.mix), custom_call_target="tpu_custom_call" | custom-call | tf_op jit(solution)/shard_map/pallas_call | solution.py:33
  (44 shorter events, 0.2 us)
Async XLA Ops:
  0.0 0.9 %copy-start.4 = (bf16[4,16,576]{2,1,0:T(8,128)(2,1)S(1)}, bf16[4,16,576]{2,1,0:T(8,128)(2,1)}, u32[]{:S(2)}) copy-start(bf16[4,16,576]{2,1,0:T(8,128)(2,1)} %queries.1) | copy-start | bytes 221188
  0.0 1.0 %copy-start.3 = (bf16[4,32,576]{2,1,0:T(8,128)(2,1)S(1)}, bf16[4,32,576]{2,1,0:T(8,128)(2,1)}, u32[]{:S(2)}) copy-start(bf16[4,32,576]{2,1,0:T(8,128)(2,1)} %cache.1) | copy-start | bytes 442372
  0.0 1.0 %copy-start.6 = (s32[4]{0:T(128)S(1)}, s32[4]{0:T(128)}, u32[]{:S(2)}) copy-start(s32[4]{0:T(128)} %lengths.1) | copy-start | bytes 52
  0.0 1.9 %copy-start.2 = (bf16[16,512,128]{2,1,0:T(8,128)(2,1)S(1)}, bf16[16,512,128]{2,1,0:T(8,128)(2,1)}, u32[]{:S(2)}) copy-start(bf16[16,512,128]{2,1,0:T(8,128)(2,1)} %w_uv.1) | copy-start | bytes 6291460
  0.0 2.0 %copy-start.5 = (bf16[4,1792]{1,0:T(4,128)(2,1)S(1)}, bf16[4,1792]{1,0:T(4,128)(2,1)}, u32[]{:S(2)}) copy-start(bf16[4,1792]{1,0:T(4,128)(2,1)} %residual.1) | copy-start | bytes 43012
  0.0 2.0 %copy-start = (s32[4,4]{1,0:T(4,128)S(1)}, s32[4,4]{1,0:T(4,128)}, u32[]{:S(2)}) copy-start(s32[4,4]{1,0:T(4,128)} %ids.3) | copy-start | bytes 196
  1.0 13.5 %slice-start.12 = ((s8[7340032]{0:T(1024)(128)(4,1)}), s8[4194304]{0:T(1024)(128)(4,1)S(1)}, s32[]{:S(2)}) async-start(s8[7340032]{0:T(1024)(128)(4,1)} %bitcast.6), calls=%async_computation.13 | async-start | bytes 8388608
  2.0 12.5 %slice-start.13 = ((s8[7340032]{0:T(1024)(128)(4,1)}), s8[3145728]{0:T(1024)(128)(4,1)S(1)}, s32[]{:S(2)}) async-start(s8[7340032]{0:T(1024)(128)(4,1)} %bitcast.6), calls=%async_computation.14 | async-start | bytes 6291456
  2.0 24.2 %slice-start.4 = ((s8[14680064]{0:T(1024)(128)(4,1)}), s8[4194304]{0:T(1024)(128)(4,1)S(1)}, s32[]{:S(2)}) async-start(s8[14680064]{0:T(1024)(128)(4,1)} %bitcast.2), calls=%async_computation.5 | async-start | bytes 8388608
  2.0 24.2 %slice-start.8 = ((s8[14680064]{0:T(1024)(128)(4,1)}), s8[4194304]{0:T(1024)(128)(4,1)S(1)}, s32[]{:S(2)}) async-start(s8[14680064]{0:T(1024)(128)(4,1)} %bitcast.4), calls=%async_computation.9 | async-start | bytes 8388608
  3.0 20.5 %copy-start.7 = (f32[1792]{0:T(1024)S(1)}, f32[1792]{0:T(1024)}, u32[]{:S(2)}) copy-start(f32[1792]{0:T(1024)} %param.18) | copy-start | bytes 21508
  3.0 20.5 %copy-start.1 = (f32[4,4]{1,0:T(4,128)S(1)}, f32[4,4]{1,0:T(4,128)}, u32[]{:S(2)}) copy-start(f32[4,4]{1,0:T(4,128)} %weights.1) | copy-start | bytes 196
  3.0 23.2 %slice-start.5 = ((s8[14680064]{0:T(1024)(128)(4,1)}), s8[4194304]{0:T(1024)(128)(4,1)S(1)}, s32[]{:S(2)}) async-start(s8[14680064]{0:T(1024)(128)(4,1)} %bitcast.2), calls=%async_computation.6 | async-start | bytes 8388608
  3.1 23.2 %slice-start.6 = ((s8[14680064]{0:T(1024)(128)(4,1)}), s8[4194304]{0:T(1024)(128)(4,1)S(1)}, s32[]{:S(2)}) async-start(s8[14680064]{0:T(1024)(128)(4,1)} %bitcast.2), calls=%async_computation.7 | async-start | bytes 8388608
  3.1 23.2 %slice-start.7 = ((s8[14680064]{0:T(1024)(128)(4,1)}), s8[2097152]{0:T(1024)(128)(4,1)S(1)}, s32[]{:S(2)}) async-start(s8[14680064]{0:T(1024)(128)(4,1)} %bitcast.2), calls=%async_computation.8 | async-start | bytes 4194304
  3.1 23.2 %slice-start.9 = ((s8[14680064]{0:T(1024)(128)(4,1)}), s8[4194304]{0:T(1024)(128)(4,1)S(1)}, s32[]{:S(2)}) async-start(s8[14680064]{0:T(1024)(128)(4,1)} %bitcast.4), calls=%async_computation.10 | async-start | bytes 8388608
  3.1 23.2 %slice-start.10 = ((s8[14680064]{0:T(1024)(128)(4,1)}), s8[4194304]{0:T(1024)(128)(4,1)S(1)}, s32[]{:S(2)}) async-start(s8[14680064]{0:T(1024)(128)(4,1)} %bitcast.4), calls=%async_computation.11 | async-start | bytes 8388608
  3.1 23.2 %slice-start.11 = ((s8[14680064]{0:T(1024)(128)(4,1)}), s8[2097152]{0:T(1024)(128)(4,1)S(1)}, s32[]{:S(2)}) async-start(s8[14680064]{0:T(1024)(128)(4,1)} %bitcast.4), calls=%async_computation.12 | async-start | bytes 4194304
  3.1 5.7 %collective-permute-start = (bf16[16,1024]{1,0:T(8,128)(2,1)S(1)}, bf16[16,1024]{1,0:T(8,128)(2,1)S(1)}, u32[]{:S(2)}, u32[]{:S(2)}) collective-permute-start(bf16[16,1024]{1,0:T(8,128)(2,1)S(1)} %shard_map.120.own), channel_id=1, source_target_pairs={{0,4},{4,0},{8,12},{12,8},{1,5},{5,1},{9,13},{13,9},{2,6},{6,2},{1... | collective-permute-start | bytes 98312 | tf_op jit(solution)/shard_map/ppermute | solution.py:382
  6.2 5.4 %collective-permute-start.1 = (bf16[16,1024]{1,0:T(8,128)(2,1)S(1)}, bf16[16,1024]{1,0:T(8,128)(2,1)S(1)}, u32[]{:S(2)}, u32[]{:S(2)}) collective-permute-start(bf16[16,1024]{1,0:T(8,128)(2,1)S(1)} %shard_map.120.own), channel_id=1, source_target_pairs={{0,8},{4,12},{8,0},{12,4},{1,9},{5,13},{9,1},{13,5},{2,10},{6,14},... | collective-permute-start | bytes 98312 | tf_op jit(solution)/shard_map/ppermute | solution.py:382
  8.8 5.7 %collective-permute-start.2 = (bf16[16,1024]{1,0:T(8,128)(2,1)S(1)}, bf16[16,1024]{1,0:T(8,128)(2,1)S(1)}, u32[]{:S(2)}, u32[]{:S(2)}) collective-permute-start(bf16[16,1024]{1,0:T(8,128)(2,1)S(1)} %shard_map.120.own), channel_id=1, source_target_pairs={{0,12},{4,8},{8,4},{12,0},{1,13},{5,9},{9,5},{13,1},{2,14},{6,10},... | collective-permute-start | bytes 98312 | tf_op jit(solution)/shard_map/ppermute | solution.py:382
  15.7 1.3 %collective-permute-start.4 = (f32[16,1792]{1,0:T(8,128)S(1)}, f32[16,1792]{1,0:T(8,128)S(1)}, u32[]{:S(2)}, u32[]{:S(2)}) collective-permute-start(f32[16,1792]{1,0:T(8,128)S(1)} %get-tuple-element.20.one), channel_id=1, source_target_pairs={{0,1},{1,0},{2,3},{3,2},{4,5},{5,4},{6,7},{7,6},{8,9},{9,8},{10,11... | collective-permute-start | bytes 344072 | tf_op jit(solution)/shard_map/ppermute | solution.py:390
  17.0 4.2 %collective-permute-start.5 = (bf16[16,1792]{1,0:T(8,128)(2,1)S(1)}, bf16[16,1792]{1,0:T(8,128)(2,1)S(1)}, u32[]{:S(2)}, u32[]{:S(2)}) collective-permute-start(bf16[16,1792]{1,0:T(8,128)(2,1)S(1)} %shard_map.123.one), channel_id=1, source_target_pairs={{0,2},{1,3},{2,0},{3,1},{4,6},{5,7},{6,4},{7,5},{8,10},{9,11},{10,... | collective-permute-start | bytes 172040 | tf_op jit(solution)/shard_map/ppermute | solution.py:393
  18.6 4.9 %collective-permute-start.3 = (bf16[32,1024]{1,0:T(8,128)(2,1)S(1)}, bf16[32,1024]{1,0:T(8,128)(2,1)S(1)}, u32[]{:S(2)}, u32[]{:S(2)}) collective-permute-start(bf16[32,1024]{1,0:T(8,128)(2,1)S(1)} %get-tuple-element.18.extra), channel_id=1, source_target_pairs={{0,16},{16,0},{1,17},{17,1},{2,18},{18,2},{3,19},{19,3},{4,20},{20... | collective-permute-start | bytes 196616 | tf_op jit(solution)/shard_map/ppermute | solution.py:391
  21.3 3.2 %collective-permute-start.6 = (bf16[16,1792]{1,0:T(8,128)(2,1)S(1)}, bf16[16,1792]{1,0:T(8,128)(2,1)S(1)}, u32[]{:S(2)}, u32[]{:S(2)}) collective-permute-start(bf16[16,1792]{1,0:T(8,128)(2,1)S(1)} %shard_map.124), channel_id=1, source_target_pairs={{0,0},{1,4},{2,8},{3,12},{4,1},{5,5},{6,9},{7,13},{8,2},{9,6},{10,... | collective-permute-start | bytes 172040 | tf_op jit(solution)/shard_map/ppermute | solution.py:395
  22.0 4.2 %collective-permute-start.7 = (bf16[16,1792]{1,0:T(8,128)(2,1)S(1)}, bf16[16,1792]{1,0:T(8,128)(2,1)S(1)}, u32[]{:S(2)}, u32[]{:S(2)}) collective-permute-start(bf16[16,1792]{1,0:T(8,128)(2,1)S(1)} %shard_map.124), channel_id=1, source_target_pairs={{0,16},{1,20},{2,24},{3,28},{4,17},{5,21},{6,25},{7,29},{8,18},{9,... | collective-permute-start | bytes 172040 | tf_op jit(solution)/shard_map/ppermute | solution.py:396
  28.4 9.6 %collective-permute-start.10 = (f32[16,2048]{1,0:T(8,128)S(1)}, f32[16,2048]{1,0:T(8,128)S(1)}, u32[]{:S(2)}, u32[]{:S(2)}) collective-permute-start(f32[16,2048]{1,0:T(8,128)S(1)} %get-tuple-element.27), channel_id=1, source_target_pairs={{0,1},{1,0},{2,3},{3,2},{4,5},{5,4},{6,7},{7,6},{8,9},{9,8},{10,11... | collective-permute-start | bytes 393224 | tf_op jit(solution)/shard_map/ppermute | solution.py:417
  29.6 1.4 %collective-permute-start.8 = (f32[16,2176]{1,0:T(8,128)S(1)}, f32[16,2176]{1,0:T(8,128)S(1)}, u32[]{:S(2)}, u32[]{:S(2)}) collective-permute-start(f32[16,2176]{1,0:T(8,128)S(1)} %get-tuple-element.24), channel_id=1, source_target_pairs={{0,1},{1,0},{2,3},{3,2},{4,5},{5,4},{6,7},{7,6},{8,9},{9,8},{10,11... | collective-permute-start | bytes 417800 | tf_op jit(solution)/shard_map/ppermute | solution.py:417
  31.0 11.6 %slice-start = ((s8[14680064]{0:T(1024)(128)(4,1)}), s8[4194304]{0:T(1024)(128)(4,1)S(1)}, s32[]{:S(2)}) async-start(s8[14680064]{0:T(1024)(128)(4,1)} %bitcast), calls=%async_computation.1 | async-start | bytes 8388608
  31.0 11.6 %slice-start.1 = ((s8[14680064]{0:T(1024)(128)(4,1)}), s8[4194304]{0:T(1024)(128)(4,1)S(1)}, s32[]{:S(2)}) async-start(s8[14680064]{0:T(1024)(128)(4,1)} %bitcast), calls=%async_computation.2 | async-start | bytes 8388608
  31.0 11.6 %slice-start.2 = ((s8[14680064]{0:T(1024)(128)(4,1)}), s8[4194304]{0:T(1024)(128)(4,1)S(1)}, s32[]{:S(2)}) async-start(s8[14680064]{0:T(1024)(128)(4,1)} %bitcast), calls=%async_computation.3 | async-start | bytes 8388608
  31.0 11.6 %slice-start.3 = ((s8[14680064]{0:T(1024)(128)(4,1)}), s8[2097152]{0:T(1024)(128)(4,1)S(1)}, s32[]{:S(2)}) async-start(s8[14680064]{0:T(1024)(128)(4,1)} %bitcast), calls=%async_computation.4 | async-start | bytes 4194304
  31.0 11.4 %collective-permute-start.9 = (bf16[16,2176]{1,0:T(8,128)(2,1)S(1)}, bf16[16,2176]{1,0:T(8,128)(2,1)S(1)}, u32[]{:S(2)}, u32[]{:S(2)}) collective-permute-start(bf16[16,2176]{1,0:T(8,128)(2,1)S(1)} %get-tuple-element.26), channel_id=1, source_target_pairs={{0,2},{1,3},{2,0},{3,1},{4,6},{5,7},{6,4},{7,5},{8,10},{9,11},{10,... | collective-permute-start | bytes 208904 | tf_op jit(solution)/shard_map/ppermute | solution.py:431
  38.1 4.3 %collective-permute-start.11 = (bf16[16,2048]{1,0:T(8,128)(2,1)S(1)}, bf16[16,2048]{1,0:T(8,128)(2,1)S(1)}, u32[]{:S(2)}, u32[]{:S(2)}) collective-permute-start(bf16[16,2048]{1,0:T(8,128)(2,1)S(1)} %get-tuple-element.29), channel_id=1, source_target_pairs={{0,2},{1,3},{2,0},{3,1},{4,6},{5,7},{6,4},{7,5},{8,10},{9,11},{10,... | collective-permute-start | bytes 196616 | tf_op jit(solution)/shard_map/ppermute | solution.py:431
  42.5 1.3 %collective-permute-start.12 = (bf16[16,2048]{1,0:T(8,128)(2,1)S(1)}, bf16[16,2048]{1,0:T(8,128)(2,1)S(1)}, u32[]{:S(2)}, u32[]{:S(2)}) collective-permute-start(bf16[16,2048]{1,0:T(8,128)(2,1)S(1)} %shard_map.130.act), channel_id=1, source_target_pairs={{0,1},{1,0},{2,3},{3,2},{4,5},{5,4},{6,7},{7,6},{8,9},{9,8},{10,11... | collective-permute-start | bytes 196616 | tf_op jit(solution)/shard_map/ppermute | solution.py:433
